TPU v7x, 512 devices: a whole 4x8x8 slice. The times are simulated.
512 devices in a mesh: ctx: 32 (over x, z_lo, core), head: 16 (over y, z_hi).
Axes of the slice: x: 4, y: 8, z: 8 (z_hi: 2, z_lo: 4; z = z_hi * 4 + z_lo), core: 2. Of those that a mesh axis runs over, the one named last changes fastest.
Arguments:
- queries: bfloat16 [4096, 8192], P('ctx', 'head'), may hold values from -9 to 9
- keys: bfloat16 [4096, 8192], P('ctx', 'head'), may hold values from -6 to 6
- values: bfloat16 [4096, 8192], P('ctx', 'head'), may hold values from -6 to 6
- d_out: bfloat16 [4096, 8192], P(('ctx', 'head')), may hold values from -6 to 6
- block_lists: int32 [32, 8], replicated, may hold values from 0 to 31, as said below
- list_counts: int32 [32], replicated, may hold values from 1 to 8, as said below
Outputs:
- attn_out: bfloat16 [4096, 8192], P('ctx', 'head')
- grad_q: bfloat16 [4096, 8192], P('ctx', 'head')
- grad_k: bfloat16 [4096, 8192], P('ctx', 'head')
- grad_v: bfloat16 [4096, 8192], P('ctx', 'head')
Inputs may be any that keep to these rules, and one draw needn't show every extreme that they name: `block_lists`: each row holds 8 distinct patch block ids; only the first list_counts entries of a row are read. Patch block p is held by index p of ctx. `list_counts`: some text block reads 8 patch blocks.
All inputs are finite; a program needn't handle non-finite values.
Results may differ from a plain program's by a relative error of at most 0.022.
Values may be sent and summed in bfloat16 or wider, within the bound.
A program may use at most 64 MiB of HBM per device.

v0:
```python
import math

import jax
import jax.numpy as jnp
from jax import lax
from jax.sharding import PartitionSpec as P

DH = 128
BLK = 128


def allowed_table(block_lists, list_counts, total_blocks):
    slot_ids = jnp.arange(block_lists.shape[1], dtype=jnp.int32)
    live_slots = slot_ids[None, :] < list_counts[:, None]
    block_ids = jnp.arange(total_blocks, dtype=jnp.int32)
    matches = (block_lists[:, :, None] == block_ids[None, None, :]) & live_slots[:, :, None]
    return jnp.any(matches, axis=1)


def tile_scores(query_rows, key_rows, scale):
    return (
        jnp.einsum("qhd,khd->hqk", query_rows, key_rows, preferred_element_type=jnp.float32) * scale
    )


def key_tile(heads_array, list_row, slot):
    return lax.dynamic_slice_in_dim(heads_array, list_row[slot] * BLK, BLK, 0)


def listed_forward(q_block, k_heads, v_heads, list_row, list_count, scale):
    heads = q_block.shape[1]

    def first_pass(slot, carry):
        running_max, running_total = carry
        scores = tile_scores(q_block, key_tile(k_heads, list_row, slot), scale)
        new_max = jnp.maximum(running_max, jnp.max(scores, axis=-1))
        running_total = running_total * jnp.exp(running_max - new_max) + jnp.sum(
            jnp.exp(scores - new_max[..., None]), axis=-1
        )
        return (new_max, running_total)

    start_max = jnp.full((heads, BLK), -jnp.inf, jnp.float32)
    start_total = jnp.zeros((heads, BLK), jnp.float32)
    row_max, row_total = lax.fori_loop(0, list_count, first_pass, (start_max, start_total))
    log_total = row_max + jnp.log(row_total)

    def second_pass(slot, acc):
        scores = tile_scores(q_block, key_tile(k_heads, list_row, slot), scale)
        weights = jnp.exp(scores - log_total[..., None]).astype(jnp.bfloat16)
        return acc + jnp.einsum(
            "hqk,khd->qhd",
            weights,
            key_tile(v_heads, list_row, slot),
            preferred_element_type=jnp.float32,
        )

    acc = lax.fori_loop(0, list_count, second_pass, jnp.zeros(q_block.shape, jnp.float32))
    return (log_total, acc.astype(jnp.bfloat16))


def listed_backward(
    q_block, d_block, k_heads, v_heads, list_row, list_count, log_total, row_delta, scale
):

    def tile_pass(slot, acc):
        key_rows = key_tile(k_heads, list_row, slot)
        scores = tile_scores(q_block, key_rows, scale)
        probs = jnp.exp(scores - log_total[..., None])
        dprobs = jnp.einsum(
            "qhd,khd->hqk",
            d_block,
            key_tile(v_heads, list_row, slot),
            preferred_element_type=jnp.float32,
        )
        dscores = (probs * (dprobs - row_delta[..., None])).astype(jnp.bfloat16)
        return acc + jnp.einsum(
            "hqk,khd->qhd", dscores, key_rows, preferred_element_type=jnp.float32
        )

    acc = lax.fori_loop(0, list_count, tile_pass, jnp.zeros(q_block.shape, jnp.float32))
    return (acc * scale).astype(jnp.bfloat16)


def shards(queries, keys, values, d_out, block_lists, list_counts):
    rows = queries.shape[0]
    heads = queries.shape[1] // DH
    scale = 1.0 / math.sqrt(DH)
    local_blocks = rows // BLK
    own_blocks = keys.shape[0] // BLK
    ctx_index = lax.axis_index("ctx")
    k_all, v_all = (
        lax.all_gather(keys, "ctx", axis=0, tiled=True),
        lax.all_gather(values, "ctx", axis=0, tiled=True),
    )
    total_blocks = k_all.shape[0] // BLK
    table = allowed_table(block_lists, list_counts, total_blocks)
    k_heads = k_all.reshape(-1, heads, DH)
    v_heads = v_all.reshape(-1, heads, DH)
    q_heads = queries.reshape(rows, heads, DH)
    d_rows = lax.all_to_all(d_out, "head", split_axis=1, concat_axis=0, tiled=True)
    d_heads = d_rows.reshape(rows, heads, DH)
    block = 0
    global_block = ctx_index * local_blocks + block
    list_row = lax.dynamic_index_in_dim(block_lists, global_block, 0, keepdims=False)
    list_count = lax.dynamic_index_in_dim(list_counts, global_block, 0, keepdims=False)
    log_block, out_block = listed_forward(q_heads, k_heads, v_heads, list_row, list_count, scale)
    delta_rows = jnp.sum(out_block.astype(jnp.float32) * d_heads.astype(jnp.float32), axis=-1).T
    block = 0
    global_block = ctx_index * local_blocks + block
    list_row = lax.dynamic_index_in_dim(block_lists, global_block, 0, keepdims=False)
    list_count = lax.dynamic_index_in_dim(list_counts, global_block, 0, keepdims=False)
    grads_list = listed_backward(
        q_heads, d_heads, k_heads, v_heads, list_row, list_count, log_block, delta_rows, scale
    )
    log_all, delta_all = (
        lax.all_gather(log_block, "ctx", axis=1, tiled=True),
        lax.all_gather(delta_rows, "ctx", axis=1, tiled=True),
    )
    own_table = lax.dynamic_slice_in_dim(table, ctx_index * own_blocks, own_blocks, 1)
    own_keys = jnp.repeat(own_table, BLK, axis=1).astype(jnp.float32)
    text_blocks = own_keys.shape[0]
    k_own = keys.reshape(-1, heads, DH)
    v_own = values.reshape(-1, heads, DH)
    d_piece = lax.all_gather(d_rows, "ctx", axis=0, tiled=True)
    count = d_piece.shape[0]
    row_block = jnp.arange(count, dtype=jnp.int32) // BLK
    one_hot = (row_block[:, None] == jnp.arange(text_blocks, dtype=jnp.int32)[None, :]).astype(
        jnp.float32
    )
    mask = jnp.dot(one_hot, own_keys) > 0.5
    q_three = lax.all_gather(queries, "ctx", axis=0, tiled=True).reshape(count, heads, DH)
    d_three = d_piece.reshape(count, heads, DH)
    scores = tile_scores(q_three, k_own, scale)
    probs = jnp.exp(jnp.where(mask[None], scores - log_all[..., None], -jnp.inf))
    weights = probs.astype(jnp.bfloat16)
    grad_values = jnp.einsum("hqk,qhd->khd", weights, d_three, preferred_element_type=jnp.float32)
    dprobs = jnp.einsum("qhd,khd->hqk", d_three, v_own, preferred_element_type=jnp.float32)
    dscores = (probs * (dprobs - delta_all[..., None])).astype(jnp.bfloat16)
    grad_keys = jnp.einsum("hqk,qhd->khd", dscores, q_three, preferred_element_type=jnp.float32)
    grad_keys, grad_values = (grad_keys, grad_values)
    attn_out = out_block.reshape(rows, heads * DH)
    grad_q = grads_list.reshape(rows, heads * DH)
    grad_k = (grad_keys * scale).astype(jnp.bfloat16).reshape(keys.shape)
    grad_v = grad_values.astype(jnp.bfloat16).reshape(values.shape)
    return (attn_out, grad_q, grad_k, grad_v)


def solution(mesh):
    return jax.shard_map(
        shards,
        mesh=mesh,
        in_specs=(
            P("ctx", "head"),
            P("ctx", "head"),
            P("ctx", "head"),
            P(("ctx", "head"), None),
            P(),
            P(),
        ),
        out_specs=(P("ctx", "head"), P("ctx", "head"), P("ctx", "head"), P("ctx", "head")),
        check_vma=False,
    )
```

profile of v0, /device:TPU:1, one launch (start us, length us, event | category | flops | bytes accessed | tf_op | source)
XLA Modules:
  0.0 356.7 jit_solution(11484293286546743806)
XLA Ops:
  7.2 1.7 copy.110
  8.9 1.7 copy.109
  10.7 1.7 copy.111
  12.4 28.8 %all_to_all.19 = bf16[8,16,512]{2,0,1:T(8,128)(2,1)} all-to-all(bf16[8,16,512]{2,0,1:T(8,128)(2,1)} %bitcast.89), channel_id=1, replica_groups=mesh['ctx'=32,'head'=16] {'head'}, dimensions={1} | all-to-all | bytes 262144 | tf_op jit(solution)/shard_map/all_to_all | solution.py:100
  41.2 0.8 copy.125
  42.0 0.9 dynamic-slice_reduce_fusion.1
  42.9 1.2 dynamic_slice.41
  44.1 1.0 copy.115
  45.1 0.7 iota_compare_fusion.3
  46.2 0.8 convolution_compare_fusion
  47.2 44.3 %all-gather.7.cloned.1.call-done = bf16[4096,512]{0,1:T(8,128)(2,1)} async-done(((bf16[128,512]{0,1:T(8,128)(2,1)}), bf16[4096,512]{0,1:T(8,128)(2,1)}) %all-gather.7.cloned.1.call-update) | async-done | bytes 4194320 | tf_op jit(solution)/shard_map/all_gather | solution.py:92
  91.5 6.3 %copy.114 = bf16[4096,4,128]{2,0,1:T(8,128)(2,1)} copy(bf16[4096,4,128]{0,2,1:T(8,128)(2,1)} %bitcast.76) | data formatting | bytes 8388608 | tf_op jit(solution)/shard_map/while | solution.py:57
  97.9 9.8 %while.32 = (s32[]{:T(128)}, f32[4,128]{1,0:T(4,128)S(1)}, f32[4,128]{1,0:T(4,128)S(1)}, s32[]{:T(128)}, s32[8]{0:T(128)S(1)}, /*index=5*/bf16[4096,4,128]{2,0,1...) while((s32[]{:T(128)}, f32[4,128]{1,0:T(4,128)S(1)}, ...), condition=%wide.region_3.4_spmd, body=%wide.region_0.3_spmd.sunk | while | flops 17040392 | bytes 813277 | solution.py:44
  98.5 0.6 dynamic_slice.73
  99.7 1.1 fusion.74
  101.5 0.6 dynamic_slice.73
  102.8 1.1 fusion.74
  104.6 0.6 dynamic_slice.73
  105.8 1.1 fusion.74
  107.6 60.3 %all-gather.5.cloned.1.call-done = bf16[4096,512]{0,1:T(8,128)(2,1)} async-done(((bf16[128,512]{0,1:T(8,128)(2,1)}), bf16[4096,512]{0,1:T(8,128)(2,1)}) %all-gather.5.cloned.1.call-update) | async-done | bytes 4194320 | tf_op jit(solution)/shard_map/all_gather | solution.py:93
  167.9 10.1 %while.33 = (s32[]{:T(128)}, f32[128,4,128]{0,2,1:T(8,128)S(1)}, s32[]{:T(128)}, s32[8]{0:T(128)S(1)}, bf16[4096,4,128]{0,2,1:T(8,128)(2,1)}, /*index=5*/bf16[40...) while((s32[]{:T(128)}, f32[128,4,128]{0,2,1:T(8,128)S(1)}, ...), condition=%wide.region_5.6_spmd, body=%wide.region_4.5_spmd.sunk | while | flops 33816584 | bytes 920801 | solution.py:57
  168.5 0.6 dynamic_slice.76
  169.7 1.3 fusion.78
  171.7 0.6 dynamic_slice.76
  172.9 1.4 fusion.78
  174.9 0.6 dynamic_slice.76
  176.1 1.3 fusion.78
  178.1 0.8 copy.138
  179.1 13.7 %while.34 = (s32[]{:T(128)}, f32[128,4,128]{0,2,1:T(8,128)S(1)}, s32[]{:T(128)}, s32[8]{0:T(128)S(1)}, bf16[4096,4,128]{2,0,1:T(8,128)(2,1)}, /*index=5*/bf16[12...) while((s32[]{:T(128)}, f32[128,4,128]{0,2,1:T(8,128)S(1)}, ...), condition=%wide.region_8.9_spmd, body=%wide.region_7.8_spmd.sunk | while | flops 50724872 | bytes 1709301 | solution.py:80
  179.7 0.6 dynamic_slice.80
  180.9 1.1 fusion.84
  182.1 1.4 fusion.85
  184.1 0.6 dynamic_slice.80
  185.3 1.1 fusion.84
  186.4 1.4 fusion.85
  188.4 0.6 dynamic_slice.80
  189.7 1.1 fusion.84
  190.8 1.4 fusion.85
  192.8 0.8 copy.139
  193.6 84.9 %all_gather.23 = f32[4,4096]{0,1:T(8,128)S(1)} all-gather(f32[4,128]{0,1:T(8,128)S(1)} %bitcast.83), channel_id=1, replica_groups=mesh['ctx'=32,'head'=16] {'ctx'}, dimensions={1}, use_global_device_ids=true | all-gather | bytes 67584 | tf_op jit(solution)/shard_map/all_gather | solution.py:117
  278.5 0.6 copy.132
  279.1 41.4 %all_gather.21 = f32[4,4096]{1,0:T(4,128)S(1)} all-gather(f32[4,128]{1,0:T(4,128)S(1)} %get-tuple-element.646), channel_id=1, replica_groups=mesh['ctx'=32,'head'=16] {'ctx'}, dimensions={1}, use_global_device_ids=true | all-gather | bytes 67584 | tf_op jit(solution)/shard_map/all_gather | solution.py:116
  320.5 7.8 %select_exponential_fusion = f32[4,4096,128]{2,1,0:T(8,128)} fusion(bf16[4096,4,128]{0,2,1:T(8,128)(2,1)} %bitcast.77, f32[4,4096]{1,0:T(4,128)S(1)} %all_gather.21, pred[4096,128]{1,0:T(8,128)(4,1)S(1)} %convolution_compare_fusion, bf16[128,512]{1,0:T(8,128)(2,1)S(1)} %copy-done.2), kind=kOutput, calls=%fused_computation.33 | convolution fusion | flops 543162368 | bytes 13303808 | tf_op jit(solution)/shard_map/qhd,khd->hqk/dot_general | solution.py:22
  328.3 6.5 %copy.129 = bf16[4096,512]{0,1:T(8,128)(2,1)} copy(bf16[4096,512]{1,0:T(8,128)(2,1)} %all-gather.11.cloned.1.call-done) | data formatting | bytes 8388608 | tf_op jit(solution)/shard_map/all_gather | solution.py:124
  334.8 5.9 %fusion.33 = bf16[4,128,128]{1,2,0:T(8,128)(2,1)S(1)} fusion(bf16[4096,4,128]{0,2,1:T(8,128)(2,1)} %bitcast.74, f32[4,4096,128]{2,1,0:T(8,128)} %select_exponential_fusion), kind=kOutput, calls=%fused_computation.40 | convolution fusion | flops 539033600 | bytes 12713984 | tf_op jit(solution)/shard_map/hqk,qhd->khd/dot_general | solution.py:136
  340.7 7.9 %fusion.32 = bf16[4,128,128]{1,2,0:T(8,128)(2,1)S(1)} fusion(bf16[4096,4,128]{0,2,1:T(8,128)(2,1)} %bitcast.78, f32[4,4096,128]{2,1,0:T(8,128)} %select_exponential_fusion, bf16[4096,4,128]{0,2,1:T(8,128)(2,1)} %bitcast.75, f32[4,4096]{1,0:T(4,128)S(1)} %copy.132, bf16[128,512]{1,0:T(8,128)(2,1)S(1)} %copy-done.1), kind=kOutput, calls=%fused_computation.39 | convolution fusion | flops 1080164352 | bytes 17104896 | tf_op jit(solution)/shard_map/hqk,qhd->khd/dot_general | solution.py:139
  348.6 0.8 copy.134
  349.4 0.8 copy.133
  (43 shorter events, 1.4 us)
Async XLA Ops:
  7.2 84.3 %all-gather.7.cloned.1.call-start = ((), (), s32[]{:S(2)}) async-start(), calls=%async_computation.2 | async-start | bytes 4325376 | tf_op jit(solution)/shard_map/all_gather | solution.py:92
  8.9 159.0 %all-gather.5.cloned.1.call-start = ((), (), s32[]{:S(2)}) async-start(), calls=%async_computation.1 | async-start | bytes 4325376 | tf_op jit(solution)/shard_map/all_gather | solution.py:93
  10.6 309.9 %all-gather.9.cloned.1.call-start = ((), (), s32[]{:S(2)}) async-start(), calls=%async_computation.3 | async-start | bytes 4325376 | tf_op jit(solution)/shard_map/all_gather | solution.py:131
  12.4 316.0 %all-gather.11.cloned.1.call-start = ((), (), s32[]{:S(2)}) async-start(), calls=%async_computation.4 | async-start | bytes 4325376 | tf_op jit(solution)/shard_map/all_gather | solution.py:124
  41.2 5.8 %copy-start = (bf16[8,16,512]{2,0,1:T(8,128)(2,1)S(1)}, bf16[8,16,512]{2,0,1:T(8,128)(2,1)}, u32[]{:S(2)}) copy-start(bf16[8,16,512]{2,0,1:T(8,128)(2,1)} %all_to_all.19) | copy-start | bytes 393220
  192.8 127.7 %copy-start.2 = (bf16[128,512]{1,0:T(8,128)(2,1)S(1)}, bf16[128,512]{1,0:T(8,128)(2,1)}, u32[]{:S(2)}) copy-start(bf16[128,512]{1,0:T(8,128)(2,1)} %param.13) | copy-start | bytes 393220
  334.8 5.9 %copy-start.1 = (bf16[128,512]{1,0:T(8,128)(2,1)S(1)}, bf16[128,512]{1,0:T(8,128)(2,1)}, u32[]{:S(2)}) copy-start(bf16[128,512]{1,0:T(8,128)(2,1)} %param.14) | copy-start | bytes 393220
Sparse Core Ops, SparseCore 0:
  10.6 80.8 all-gather.6
  94.1 73.7 all-gather.4
  170.5 73.7 all-gather.8
  246.3 66.3 all-gather.10
where the time goes:
time: 359 us; the launch traced here: 357 us
  blocking collectives  155 us (43%)
  waiting for transfers between devices  105 us (29%)
  matrix products  37.4 us (10%)
  local copies, waits for them, and re-layouts  31.3 us (9%)
  between operations  13.9 us (4%)
  loops' own time  13 us (4%)
    all_gather x1, blocking collectives, shards(): lax.all_gather(delta_rows, 'ctx', axis=1, tiled=True)  84.9 us
    all_gather x1, waiting for transfers between devices, shards(): lax.all_gather(values, 'ctx', axis=0, tiled=True)  60.3 us
    all_gather x1, waiting for transfers between devices, shards(): lax.all_gather(keys, 'ctx', axis=0, tiled=True)  44.3 us
    all_gather x1, blocking collectives, shards(): lax.all_gather(log_block, 'ctx', axis=1, tiled=True)  41.4 us
    all_to_all x1, blocking collectives, shards(): lax.all_to_all(d_out, 'head', split_axis=1, concat_axis=0, tiled=True)  28.8 us
    dot_general x7, matrix products, tile_scores(): jnp.einsum('qhd,khd->hqk', query_rows, key_rows, preferred_element_type=j...  14.6 us
    dot_general x1, matrix products, shards(): jnp.einsum('hqk,qhd->khd', dscores, q_three, preferred_element_type=jnp.f...  7.87 us
    unnamed x13, local copies, waits for them, and re-layouts  7.46 us
  transfers between devices with their start and end apart: 4, of which 2 were waited for; matrix products, arithmetic and copies ran while one was open for 13% of the time, Pallas kernels for 0%

commit v1 on v0

v1 whole, which is shorter than its diff:
```python
import functools
import math

import jax
import jax.numpy as jnp
from jax import lax
from jax.experimental import pallas as pl
from jax.experimental.pallas import tpu as pltpu
from jax.sharding import PartitionSpec as P

DH = 128
BLK = 128
MAXB = 8
NX, NZ, NC = 4, 4, 2
NPOS = NX * NZ * NC
GROUP = 4
MESH = pl.DeviceIdType.MESH
BF16, F32 = jnp.bfloat16, jnp.float32
SCALE = 1.0 / math.sqrt(DH)
LOG2E = math.log2(math.e)


def coords():
    i = lax.axis_index("ctx")
    return i // (NZ * NC), (i // NC) % NZ, i % NC


def ctx_id(x, z, c):
    return {"ctx": x * (NZ * NC) + z * NC + c}


def slot_of(x, z, c):
    return c * (NX * NZ) + x * NZ + z


def send(src, dst, send_sem, recv_sem, device):
    copy = pltpu.make_async_remote_copy(
        src_ref=src, dst_ref=dst, send_sem=send_sem, recv_sem=recv_sem,
        device_id=device, device_id_type=MESH,
    )
    copy.start()
    return copy


def enter(partners):
    barrier = pltpu.get_barrier_semaphore()
    for partner in partners:
        pl.semaphore_signal(barrier, inc=1, device_id=partner, device_id_type=MESH)
    pl.semaphore_wait(barrier, len(partners))


def gather_kernel(
    heads, q, k, v, d, kh, vh, qh, dh, d_rows,
    z_send, z_recv, x_send, x_recv, c_send, c_recv, h_send, h_recv, local,
):
    x, z, c = coords()
    g = lax.axis_index("head")
    right, left = (x + 1) % NX, (x + 3) % NX
    to_right, to_left = ctx_id(right, z, c), ctx_id(left, z, c)
    sibling = ctx_id(x, z, 1 - c)
    z_of = [(z + r) % NZ for r in range(NZ)]
    enter(
        [ctx_id(x, z_of[r], c) for r in range(1, NZ)]
        + [to_right, to_left, sibling]
        + [{"head": (g + r) % heads} for r in range(1, heads)]
    )
    mine = slot_of(x, z, c)
    copies = []

    def columns(ref, head):
        return ref.at[:, pl.ds(pl.multiple_of(head * DH, DH), DH)]

    def spread(index, ref, dst):
        got = []
        for r in range(1, NZ):
            copies.append(send(
                columns(ref, z_of[r]), dst, z_send.at[index, r], z_recv.at[index, r],
                ctx_id(x, z_of[r], c),
            ))
            got.append(copies[-1])
        own = pltpu.make_async_copy(columns(ref, z), dst, local.at[index])
        own.start()
        return got, own

    def settle(parts):
        got, own = parts
        own.wait()
        for copy in got:
            copy.wait_recv()

    k_parts = spread(0, k, kh.at[mine])
    v_parts = spread(1, v, vh.at[mine])
    d_parts = []
    for r in range(1, heads):
        there = (g + r) % heads
        d_parts.append(send(
            d.at[:, pl.ds(pl.multiple_of(there * (GROUP * DH), GROUP * DH), GROUP * DH)],
            d_rows.at[g], h_send.at[r], h_recv.at[r], {"head": there},
        ))
    d_own = pltpu.make_async_copy(
        d.at[:, pl.ds(pl.multiple_of(g * (GROUP * DH), GROUP * DH), GROUP * DH)],
        d_rows.at[g], local.at[4],
    )
    d_own.start()
    copies.extend(d_parts)
    q_parts = spread(2, q, qh.at[z])

    def shard(ref, chip, core):
        return ref.at[pl.ds(core * (NX * NZ) + chip * NZ, NZ)]

    def pass_on(index, ref, chip, device, sems, slot):
        part = shard(ref, chip, c)
        copies.append(send(
            part, part, sems[0].at[index, slot], sems[1].at[index, slot], device,
        ))
        return copies[-1]

    x_sems, c_sems = (x_send, x_recv), (c_send, c_recv)
    settle(k_parts)
    k_right = pass_on(0, kh, x, to_right, x_sems, 0)
    k_left = pass_on(0, kh, x, to_left, x_sems, 1)
    sib = [pass_on(0, kh, x, sibling, c_sems, 0)]
    settle(v_parts)
    v_left = pass_on(1, vh, x, to_left, x_sems, 1)
    v_right = pass_on(1, vh, x, to_right, x_sems, 0)
    sib.append(pass_on(1, vh, x, sibling, c_sems, 0))
    k_right.wait_recv()
    k_far = pass_on(0, kh, left, to_right, x_sems, 2)
    sib.append(pass_on(0, kh, left, sibling, c_sems, 1))
    v_left.wait_recv()
    v_far = pass_on(1, vh, right, to_left, x_sems, 2)
    sib.append(pass_on(1, vh, right, sibling, c_sems, 1))
    k_left.wait_recv()
    sib.append(pass_on(0, kh, right, sibling, c_sems, 2))
    v_right.wait_recv()
    sib.append(pass_on(1, vh, left, sibling, c_sems, 2))
    d_own.wait()
    for copy in d_parts:
        copy.wait_recv()
    dz = []
    for r in range(1, NZ):
        head = pl.multiple_of(z_of[r] * DH, DH)
        copies.append(send(
            d_rows.at[:, :, pl.ds(head, DH)], dh.at[z], z_send.at[3, r], z_recv.at[3, r],
            ctx_id(x, z_of[r], c),
        ))
        dz.append(copies[-1])
    dz_own = pltpu.make_async_copy(
        d_rows.at[:, :, pl.ds(pl.multiple_of(z * DH, DH), DH)], dh.at[z], local.at[3]
    )
    dz_own.start()
    far = (x + 2) % NX
    k_far.wait_recv()
    sib.append(pass_on(0, kh, far, sibling, c_sems, 3))
    v_far.wait_recv()
    sib.append(pass_on(1, vh, far, sibling, c_sems, 3))
    settle(q_parts)
    settle((dz, dz_own))
    for copy in sib:
        copy.wait_recv()
    for copy in copies:
        copy.wait_send()


def attend_kernel(
    lists, counts, q, k, v, d, attn, grad_q, grad_k, grad_v, k_acc, v_acc, k_rows, v_rows
):
    x, z, c = coords()
    k_acc[...] = jnp.zeros_like(k_acc)
    v_acc[...] = jnp.zeros_like(v_acc)
    contract_last = (((1,), (1,)), ((), ()))
    contract_first = (((0,), (0,)), ((), ()))

    def text_block(b, _):
        t = x * (NZ * NC) + b * NC + c
        count = counts[t]
        slots = []
        for j in range(MAXB):
            p = lists[t, j]
            slot = slot_of(p // (NZ * NC), (p // NC) % NZ, p % NC)
            slots.append(slot)
            k_rows[pl.ds(j * BLK, BLK), :] = k[slot]
            v_rows[pl.ds(j * BLK, BLK), :] = v[slot]
        qb, db = q[b], d[b]
        keys, vals = k_rows[...], v_rows[...]
        scores = lax.dot_general(keys, qb, contract_last, preferred_element_type=F32)
        live = lax.broadcasted_iota(jnp.int32, scores.shape, 0) < count * BLK
        scores = jnp.where(live, scores, -jnp.inf)
        top = jnp.max(scores, axis=0, keepdims=True)
        e = jnp.exp2((scores - top) * (SCALE * LOG2E))
        total = jnp.sum(e, axis=0, keepdims=True)
        probs = e * (1.0 / total)
        weights = probs.astype(BF16)
        dprobs = lax.dot_general(vals, db, contract_last, preferred_element_type=F32)
        delta = jnp.sum(weights.astype(F32) * dprobs, axis=0, keepdims=True)
        dscores = (probs * (dprobs - delta)).astype(BF16)
        attn[b] = lax.dot_general(
            weights, vals, contract_first, preferred_element_type=F32
        ).astype(BF16)
        grad_q[b] = (
            lax.dot_general(dscores, keys, contract_first, preferred_element_type=F32) * SCALE
        ).astype(BF16)
        dv = jnp.dot(weights, db, preferred_element_type=F32)
        dk = jnp.dot(dscores, qb, preferred_element_type=F32)
        for j in range(MAXB):
            v_acc[slots[j]] += dv[j * BLK : (j + 1) * BLK]
            k_acc[slots[j]] += dk[j * BLK : (j + 1) * BLK]
        return 0

    lax.fori_loop(0, NZ, text_block, 0)
    grad_k[...] = (k_acc[...] * SCALE).astype(BF16)
    grad_v[...] = v_acc[...].astype(BF16)


def scatter_kernel(
    attn_in, gq_in, dk_in, dv_in, attn, grad_q, grad_k, grad_v,
    sib_in, sums, x_in, final,
    z_send, z_recv, x_send, x_recv, c_send, c_recv, local,
):
    x, z, c = coords()
    right, left, far = (x + 1) % NX, (x + 3) % NX, (x + 2) % NX
    to_right, to_left = ctx_id(right, z, c), ctx_id(left, z, c)
    sibling = ctx_id(x, z, 1 - c)
    z_of = [(z + r) % NZ for r in range(NZ)]
    enter([ctx_id(x, z_of[r], c) for r in range(1, NZ)] + [to_right, to_left, sibling])
    copies = []

    def columns(ref):
        return ref.at[:, pl.ds(pl.multiple_of(z * DH, DH), DH)]

    def spread(index, ref, out):
        got = []
        for r in range(1, NZ):
            copies.append(send(
                ref.at[z_of[r]], columns(out), z_send.at[index, r], z_recv.at[index, r],
                ctx_id(x, z_of[r], c),
            ))
            got.append(copies[-1])
        own = pltpu.make_async_copy(ref.at[z], columns(out), local.at[index])
        own.start()
        return got, own

    partial = (dk_in, dv_in)
    order = ((far, left, right, x), (far, right, left, x))
    sib = [[None] * NX, [None] * NX]
    for n in range(NX):
        for i in range(2):
            chip = order[i][n]
            sib[i][n] = send(
                partial[i].at[pl.ds((1 - c) * (NX * NZ) + chip * NZ, NZ)],
                sib_in.at[i, n], c_send.at[i, n], c_recv.at[i, n], sibling,
            )
            copies.append(sib[i][n])
    parts = [spread(0, attn_in, attn), spread(1, gq_in, grad_q)]
    forward, back = (to_right, to_left), (to_left, to_right)

    def add(i, n, others, out):
        sib[i][n].wait_recv()
        base = c * (NX * NZ) + order[i][n] * NZ

        def block(j, _):
            total = partial[i][base + j].astype(F32) + sib_in[i, n, j].astype(F32)
            for other in others:
                total = total + x_in[i, other, j].astype(F32)
            out[j] = total.astype(BF16)
            return 0

        lax.fori_loop(0, NZ, block, 0)

    def ship(i, n, device):
        copies.append(send(
            sums.at[i, n], x_in.at[i, n], x_send.at[i, n], x_recv.at[i, n], device
        ))
        return copies[-1]

    moves = [[], []]
    for i in range(2):
        add(i, 0, (), sums.at[i, 0])
        moves[i].append(ship(i, 0, forward[i]))
    for i in range(2):
        add(i, 1, (), sums.at[i, 1])
        moves[i].append(ship(i, 1, back[i]))
    for i in range(2):
        moves[i][0].wait_recv()
        add(i, 2, (0,), sums.at[i, 2])
        moves[i].append(ship(i, 2, forward[i]))
    for i in range(2):
        moves[i][1].wait_recv()
        moves[i][2].wait_recv()
        add(i, 3, (1, 2), final.at[i])
        parts.append(spread(2 + i, final.at[i], (grad_k, grad_v)[i]))
    for got, own in parts:
        own.wait()
        for copy in got:
            copy.wait_recv()
    for copy in copies:
        copy.wait_send()


def shards(queries, keys, values, d_out, block_lists, list_counts):
    heads = lax.axis_size("head")
    hbm = pl.BlockSpec(memory_space=pl.ANY)
    vmem = pl.BlockSpec(memory_space=pltpu.VMEM)
    smem = pl.BlockSpec(memory_space=pltpu.SMEM)
    dma = pltpu.SemaphoreType.DMA
    blocks = jax.ShapeDtypeStruct((NPOS, BLK, DH), BF16)
    mine = jax.ShapeDtypeStruct((NZ, BLK, DH), BF16)
    rows = BLK // heads
    kh, vh, qh, dh, _ = pl.pallas_call(
        functools.partial(gather_kernel, heads),
        out_shape=(
            blocks, blocks, mine,
            jax.ShapeDtypeStruct((NZ, heads, rows, DH), BF16),
            jax.ShapeDtypeStruct((heads, rows, GROUP * DH), BF16),
        ),
        in_specs=[hbm] * 4,
        out_specs=[hbm] * 5,
        scratch_shapes=[
            dma((4, NZ)), dma((4, NZ)), dma((2, 3)), dma((2, 3)), dma((2, NX)), dma((2, NX)),
            dma((heads,)), dma((heads,)), dma((5,)),
        ],
        compiler_params=pltpu.CompilerParams(collective_id=0, has_side_effects=True),
        name="gather",
    )(queries, keys, values, d_out)
    attn_b, gq_b, dk_b, dv_b = pl.pallas_call(
        attend_kernel,
        out_shape=(mine, mine, blocks, blocks),
        in_specs=[smem, smem] + [vmem] * 4,
        out_specs=[vmem] * 4,
        scratch_shapes=[
            pltpu.VMEM((NPOS, BLK, DH), F32), pltpu.VMEM((NPOS, BLK, DH), F32),
            pltpu.VMEM((MAXB * BLK, DH), BF16), pltpu.VMEM((MAXB * BLK, DH), BF16),
        ],
        compiler_params=pltpu.CompilerParams(vmem_limit_bytes=48 << 20),
        name="attend",
    )(block_lists, list_counts, qh, kh, vh, dh.reshape(NZ, BLK, DH))
    out = jax.ShapeDtypeStruct((BLK, GROUP * DH), BF16)
    return pl.pallas_call(
        scatter_kernel,
        out_shape=(out,) * 4,
        in_specs=[vmem] * 4,
        out_specs=[hbm] * 4,
        scratch_shapes=[
            pltpu.VMEM((2, NX, NZ, BLK, DH), BF16),
            pltpu.VMEM((2, 3, NZ, BLK, DH), BF16),
            pltpu.VMEM((2, 3, NZ, BLK, DH), BF16),
            pltpu.VMEM((2, NZ, BLK, DH), BF16),
            dma((4, NZ)), dma((4, NZ)), dma((2, 3)), dma((2, 3)), dma((2, NX)), dma((2, NX)),
            dma((4,)),
        ],
        compiler_params=pltpu.CompilerParams(
            collective_id=1, has_side_effects=True, vmem_limit_bytes=48 << 20
        ),
        name="scatter",
    )(attn_b, gq_b, dk_b, dv_b)


def solution(mesh):
    spec = P("ctx", "head")
    return jax.shard_map(
        shards,
        mesh=mesh,
        in_specs=(spec, spec, spec, P(("ctx", "head"), None), P(), P()),
        out_specs=(spec,) * 4,
        check_vma=False,
    )
```

time: 359 us -> 76.9 us (0.21)
  blocking collectives: 155 us -> 0 us
  waiting for transfers between devices: 105 us -> 0 us
  Pallas kernels: 0 us -> 67.4 us
  matrix products: 37.4 us -> 0 us
  local copies, waits for them, and re-layouts: 31.3 us -> 8.29 us
  between operations: 13.9 us -> 0.67 us
  loops' own time: 13 us -> 0 us
    all_gather x2 -> x0, blocking collectives: 126 us -> none  [the longest x1 84.9 us: shards(): lax.all_gather(delta_rows, 'ctx', axis=1, tiled=True)]
    all_gather x4 -> x0, waiting for transfers between devices: 105 us -> none  [the longest x1 60.3 us: shards(): lax.all_gather(values, 'ctx', axis=0, tiled=True)]
    pallas_call x0 -> x3, Pallas kernels: none -> 67.4 us  [the longest x1 41.2 us: shards(): pl.pallas_call(functools.partial(gather_kernel, heads), out_shape=(blocks...]
    dot_general x16 -> x0, matrix products: 37.4 us -> none  [the longest x7 14.6 us: tile_scores(): jnp.einsum('qhd,khd->hqk', query_rows, key_rows, preferred_element_type=j...]
    all_to_all x1 -> x0, blocking collectives: 28.8 us -> none  [shards(): lax.all_to_all(d_out, 'head', split_axis=1, concat_axis=0, tiled=True)]
    another operation x3 -> x0, loops' own time: 13 us -> none  [the longest x1 4.35 us: listed_forward(): lax.fori_loop(0, list_count, first_pass, (start_max, start_total))]
    dynamic_slice x12 -> x0, local copies, waits for them, and re-layouts: 7.55 us -> none  [the longest x9 5.28 us: key_tile(): return lax.dynamic_slice_in_dim(heads_array, list_row[slot] * BLK, BLK, 0)]
    while x7 -> x0, local copies, waits for them, and re-layouts: 7.46 us -> none  [the longest x2 7.37 us: listed_forward(): lax.fori_loop(0, list_count, second_pass, jnp.zeros(q_block.shape, jnp.fl...]
  transfers between devices with their start and end apart: 4 -> 0, of which waited for: 2 -> 0; matrix products, arithmetic and copies ran while one was open for 13% -> 0% of each run, Pallas kernels for 0% -> 0%
where the time goes in v1:
time: 76.9 us; the launch traced here: 76.3 us
  Pallas kernels  67.4 us (88%)
  local copies, waits for them, and re-layouts  8.29 us (11%)
    pallas_call x1, Pallas kernels, shards(): pl.pallas_call(functools.partial(gather_kernel, heads), out_shape=(blocks...  41.2 us
    pallas_call x1, Pallas kernels, shards(): pl.pallas_call(scatter_kernel, out_shape=(out,) * 4, in_specs=[vmem] * 4,...  20.6 us
    unnamed x15, local copies, waits for them, and re-layouts  8.29 us
    pallas_call x1, Pallas kernels, shards(): pl.pallas_call(attend_kernel, out_shape=(mine, mine, blocks, blocks), in_...  5.61 us

profile of v1, /device:TPU:1, one launch (start us, length us, event | category | flops | bytes accessed | tf_op | source)
XLA Modules:
  0.0 76.3 jit_solution(4770600500537435513)
XLA Ops:
  0.6 0.8 copy.10.lists
  1.4 41.2 %gather.1 = (bf16[32,128,128]{2,1,0:T(8,128)(2,1)}, bf16[32,128,128]{2,1,0:T(8,128)(2,1)}, bf16[4,128,128]{2,1,0:T(8,128)(2,1)}, bf16[4,16,8,128]{3,2,1,0:T(8,128)(2,1)}, bf16[16,8,512]{2,1,0:T(8,128)(2,1)}) custom-call(bf16[128,512]{1,0:T(8,128)(2,1)} %q.1, bf16[128,512]{1,0:T(8,128)(2,1)} %k.1, bf16[128,512]{1,0:T(8,128)(2,1)} %v.1, bf16[8,8192]{1,0:T(8,128)(2,1)} %d.1), custom_call_target="tpu_custom_call" | custom-call | tf_op jit(solution)/shard_map/gather/pallas_call | solution.py:309
  42.6 0.0 copy-start.4
  42.6 0.6 copy-done.4
  43.3 0.0 copy-start
  43.3 1.2 %copy-done = bf16[32,128,128]{2,1,0:T(8,128)(2,1)S(1)} copy-done((bf16[32,128,128]{2,1,0:T(8,128)(2,1)S(1)}, bf16[32,128,128]{2,1,0:T(8,128)(2,1)}, u32[]{:S(2)}) %copy-start) | copy-done | bytes 1048600
  44.5 0.0 copy-start.1
  44.5 1.2 %copy-done.1 = bf16[32,128,128]{2,1,0:T(8,128)(2,1)S(1)} copy-done((bf16[32,128,128]{2,1,0:T(8,128)(2,1)S(1)}, bf16[32,128,128]{2,1,0:T(8,128)(2,1)}, u32[]{:S(2)}) %copy-start.1) | copy-done | bytes 1048600
  45.7 0.0 copy-start.2
  45.7 0.9 %copy-done.2 = bf16[4,128,128]{2,1,0:T(8,128)(2,1)S(1)} copy-done((bf16[4,128,128]{2,1,0:T(8,128)(2,1)S(1)}, bf16[4,128,128]{2,1,0:T(8,128)(2,1)}, u32[]{:S(2)}) %copy-start.2) | copy-done | bytes 131096
  46.6 0.0 copy-start.3
  46.6 0.9 %copy-done.3 = bf16[4,16,8,128]{3,2,1,0:T(8,128)(2,1)S(1)} copy-done((bf16[4,16,8,128]{3,2,1,0:T(8,128)(2,1)S(1)}, bf16[4,16,8,128]{3,2,1,0:T(8,128)(2,1)}, u32[]{:S(2)}) %copy-start.3) | copy-done | bytes 131096
  47.5 5.6 %attend.1 = (bf16[4,128,128]{2,1,0:T(8,128)(2,1)S(1)}, bf16[4,128,128]{2,1,0:T(8,128)(2,1)S(1)}, bf16[32,128,128]{2,1,0:T(8,128)(2,1)S(1)}, bf16[32,128,128]{2,1,0:T(8,128)(2,1)S(1)}) custom-call(s32[32,8]{1,0:T(8,128)S(1)} %copy.10.lists, s32[32]{0:T(128)S(1)} %copy-done.4, bf16[4,128,128]{2,1,0:T(8,128)(2,1)S(1)} %copy-done.2, ...), custom_call_target="tpu_custom_call" | custom-call | tf_op jit(solution)/shard_map/attend/pallas_call | solution.py:325
  53.1 20.6 %scatter.1 = (bf16[128,512]{1,0:T(8,128)(2,1)S(1)}, bf16[128,512]{1,0:T(8,128)(2,1)S(1)}, bf16[128,512]{1,0:T(8,128)(2,1)S(1)}, bf16[128,512]{1,0:T(8,128)(2,1)S(1)}) custom-call(bf16[4,128,128]{2,1,0:T(8,128)(2,1)S(1)} %get-tuple-element.16.attn_in, bf16[4,128,128]{2,1,0:T(8,128)(2,1)S(1)} %get-tuple-element.17.gq_in, ...), custom_call_target="tpu_custom_call" | custom-call | tf_op jit(solution)/shard_map/scatter/pallas_call | solution.py:338
  73.7 0.7 copy.15
  74.4 0.7 copy.16
  75.0 0.7 copy.17
  75.7 0.7 copy.18
Async XLA Ops:
  42.6 0.7 copy-start.4
  43.3 1.2 %copy-start = (bf16[32,128,128]{2,1,0:T(8,128)(2,1)S(1)}, bf16[32,128,128]{2,1,0:T(8,128)(2,1)}, u32[]{:S(2)}) copy-start(bf16[32,128,128]{2,1,0:T(8,128)(2,1)} %get-tuple-element.13.k) | copy-start | bytes 3145732
  44.5 1.2 %copy-start.1 = (bf16[32,128,128]{2,1,0:T(8,128)(2,1)S(1)}, bf16[32,128,128]{2,1,0:T(8,128)(2,1)}, u32[]{:S(2)}) copy-start(bf16[32,128,128]{2,1,0:T(8,128)(2,1)} %get-tuple-element.14.v) | copy-start | bytes 3145732
  45.7 0.9 %copy-start.2 = (bf16[4,128,128]{2,1,0:T(8,128)(2,1)S(1)}, bf16[4,128,128]{2,1,0:T(8,128)(2,1)}, u32[]{:S(2)}) copy-start(bf16[4,128,128]{2,1,0:T(8,128)(2,1)} %get-tuple-element.12.q) | copy-start | bytes 393220
  46.6 0.9 %copy-start.3 = (bf16[4,16,8,128]{3,2,1,0:T(8,128)(2,1)S(1)}, bf16[4,16,8,128]{3,2,1,0:T(8,128)(2,1)}, u32[]{:S(2)}) copy-start(bf16[4,16,8,128]{3,2,1,0:T(8,128)(2,1)} %get-tuple-element.15) | copy-start | bytes 393220

commit v2 on v0

v2 whole, which is shorter than its diff:
```python
import math

import jax
import jax.numpy as jnp
from jax import lax
from jax.experimental import pallas as pl
from jax.experimental.pallas import tpu as pltpu
from jax.sharding import PartitionSpec as P

DH = 128
BLK = 128
MAXB = 8
NX, NY, NZ, NC = 4, 8, 4, 2
NPOS = NX * NZ * NC
GROUP = 4
MESH = pl.DeviceIdType.MESH
BF16, F32 = jnp.bfloat16, jnp.float32
SCALE = 1.0 / math.sqrt(DH)
LOG2E = math.log2(math.e)
LAST = (((1,), (1,)), ((), ()))
FIRST = (((0,), (0,)), ((), ()))


def coords():
    i = lax.axis_index("ctx")
    return i // (NZ * NC), (i // NC) % NZ, i % NC


def head_coords():
    g = lax.axis_index("head")
    return g // 2, g % 2


def z_order(z):
    return [z, z + 1 - 2 * (z % 2), (z + 2) % NZ, NZ - 1 - z]


def ctx_id(x, z, c):
    return {"ctx": x * (NZ * NC) + z * NC + c}


def slot_of(x, z, c):
    return c * (NX * NZ) + x * NZ + z


def send(src, dst, send_sem, recv_sem, device):
    copy = pltpu.make_async_remote_copy(
        src_ref=src, dst_ref=dst, send_sem=send_sem, recv_sem=recv_sem,
        device_id=device, device_id_type=MESH,
    )
    copy.start()
    return copy


def columns(ref, start, width):
    return ref.at[:, pl.ds(pl.multiple_of(start, DH), width)]


def kernel(
    lists, counts, q, k, v, d, attn, grad_q, grad_k, grad_v,
    kh, vh, qh, dh, d_rows, where, k_rows, v_rows, probs, weights, dscores, d_cat, own_out,
    lhs, give, sib_in, sums, x_in, final,
    z_send, z_recv, x_send, x_recv, c_send, c_recv, y_send, y_recv, d_send, d_recv,
    oz_send, oz_recv, ox_send, ox_recv, oc_send, oc_recv, local,
):
    x, z, c = coords()
    y, h = head_coords()
    right, left, far = (x + 1) % NX, (x + 3) % NX, (x + 2) % NX
    to_right, to_left, sibling = ctx_id(right, z, c), ctx_id(left, z, c), ctx_id(x, z, 1 - c)
    z_of = z_order(z)

    def z_id(n, flip):
        return {**ctx_id(x, z_of[n], c), "head": 2 * y + (h if flip == 0 else 1 - h)}

    def y_id(r):
        return {"head": 2 * ((y + r) % NY) + h}

    partners = (
        [ctx_id(x, z_of[n], c) for n in range(1, NZ)]
        + [to_right, to_left, sibling]
        + [y_id(r) for r in range(1, NY)]
        + [z_id(n, 1) for n in range(NZ)]
    )
    barrier = pltpu.get_barrier_semaphore()
    for partner in partners:
        pl.semaphore_signal(barrier, inc=1, device_id=partner, device_id_type=MESH)
    pl.semaphore_wait(barrier, len(partners))
    copies = []

    def go(*args):
        copies.append(send(*args))
        return copies[-1]

    def keep(src, dst, sem):
        copy = pltpu.make_async_copy(src, dst, sem)
        copy.start()
        return copy

    ins, outs = (k, v, q), (kh, vh, qh)

    def across(i, n):
        place = slot_of(x, z, c) if i < 2 else z
        return go(
            columns(ins[i], z_of[n] * DH, DH), outs[i].at[place],
            z_send.at[i, n], z_recv.at[i, n], ctx_id(x, z_of[n], c),
        )

    def along(i, n, role):
        to = (to_right, to_left, (to_right, to_left)[i])[role]
        chip = (x, x, (left, right)[i])[role]
        dst = outs[i].at[slot_of(chip, z_of[n], c)]
        src = columns(ins[i], z * DH, DH) if role < 2 and n == 0 else dst
        return go(src, dst, x_send.at[i, role, n], x_recv.at[i, role, n], to)

    def over(i, m, chip):
        part = outs[i].at[pl.ds(c * (NX * NZ) + chip * NZ, NZ)]
        return go(part, part, c_send.at[i, m], c_recv.at[i, m], sibling)

    zs = [[None] * NZ for _ in range(3)]
    xs = [[[None] * NZ for _ in range(3)] for _ in range(2)]
    sib = [[], []]

    def own_block(i, n):
        if n > 0:
            zs[i][n].wait_recv()
        for role in range(2):
            xs[i][role][n] = along(i, n, role)

    def pass_on(i, n):
        xs[i][i][n].wait_recv()
        xs[i][2][n] = along(i, n, 2)

    def rest(i):
        other = 1 - i
        for n in range(NZ):
            xs[i][other][n].wait_recv()
        sib[i].append(over(i, 2, (right, left)[i]))
        for n in range(NZ):
            xs[i][2][n].wait_recv()
        sib[i].append(over(i, 3, far))

    for i in range(2):
        for n in range(1, NZ):
            zs[i][n] = across(i, n)
        own_block(i, 0)
    own = [
        keep(columns(ins[i], z * DH, DH), outs[i].at[slot_of(x, z, c) if i < 2 else z], local.at[i])
        for i in range(3)
    ]
    ys = [
        go(
            columns(d, ((y + r) % NY) * (2 * GROUP * DH), 2 * GROUP * DH), d_rows.at[y],
            y_send.at[r], y_recv.at[r], y_id(r),
        )
        for r in range(1, NY)
    ]
    d_own = keep(columns(d, y * (2 * GROUP * DH), 2 * GROUP * DH), d_rows.at[y], local.at[3])
    for n in range(1, NZ):
        zs[2][n] = across(2, n)

    def text_of(b):
        return x * (NZ * NC) + b * NC + c

    for b in range(NZ):
        t = text_of(b)
        count = counts[t]
        live = [jnp.where(j < count, lists[j, t], -1) for j in range(MAXB)]

        def find(pos, _):
            p = ((pos // NZ) % NX) * (NZ * NC) + (pos % NZ) * NC + pos // (NX * NZ)
            at = jnp.int32(MAXB)
            for j in range(MAXB):
                at = jnp.where(live[j] == p, j, at)
            where[b, pos] = at
            return 0

        lax.fori_loop(0, NPOS, find, 0)
        weights[b, MAXB] = jnp.zeros((BLK, BLK), BF16)
        dscores[b, MAXB] = jnp.zeros((BLK, BLK), BF16)

    own_block(0, 1)
    pass_on(0, 0)
    own_block(0, 2)
    pass_on(0, 1)
    own_block(0, 3)
    own[0].wait()
    sib[0].append(over(0, 0, x))
    pass_on(0, 2)
    own_block(1, 1)
    pass_on(0, 3)
    sib[0].append(over(0, 1, left))
    pass_on(1, 0)
    own_block(1, 2)
    d_own.wait()
    for copy in ys:
        copy.wait_recv()
    ds = []
    for flip in range(2):
        group = h if flip == 0 else 1 - h
        for n in range(NZ):
            part = d_rows.at[:, :, pl.ds(pl.multiple_of((group * GROUP + z_of[n]) * DH, DH), DH)]
            dst = dh.at[z, :, h]
            if flip == 0 and n == 0:
                d_keep = keep(part, dst, local.at[4])
            else:
                m = flip * NZ + n
                ds.append(go(part, dst, d_send.at[m], d_recv.at[m], z_id(n, flip)))
    own_block(1, 3)
    own[1].wait()
    sib[1].append(over(1, 0, x))
    pass_on(1, 1)
    rest(0)
    own[2].wait()
    for copy in zs[2][1:] + sib[0]:
        copy.wait_recv()

    def listed(ref, b, out):
        t = text_of(b)
        for j in range(MAXB):
            p = lists[j, t]
            out[pl.ds(j * BLK, BLK), :] = ref[slot_of(p // (NZ * NC), (p // NC) % NZ, p % NC)]

    def softmax(b):
        listed(kh, b, k_rows.at[b])
        scores = lax.dot_general(k_rows[b], qh[b], LAST, preferred_element_type=F32)
        row = lax.broadcasted_iota(jnp.int32, scores.shape, 0)
        scores = jnp.where(row < counts[text_of(b)] * BLK, scores, -jnp.inf)
        top = jnp.max(scores, axis=0, keepdims=True)
        e = jnp.exp2((scores - top) * (SCALE * LOG2E))
        p = e * (1.0 / jnp.sum(e, axis=0, keepdims=True))
        probs[b] = p
        weights[b, :MAXB] = p.astype(BF16).reshape(MAXB, BLK, BLK)

    softmax(0)
    pass_on(1, 2)
    softmax(1)
    pass_on(1, 3)
    sib[1].append(over(1, 1, right))
    softmax(2)
    rest(1)
    softmax(3)
    d_keep.wait()
    for copy in sib[1] + ds:
        copy.wait_recv()

    parts = []

    def spread(m, src, out):
        for n in range(1, NZ):
            parts.append(go(
                src.at[z_of[n]], columns(out, z * DH, DH), oz_send.at[m, n], oz_recv.at[m, n],
                ctx_id(x, z_of[n], c),
            ))
        return keep(src.at[z], columns(out, z * DH, DH), local.at[5 + m])

    def backward(b, _):
        db = dh[b].astype(F32).reshape(BLK, DH).astype(BF16)
        d_cat[b] = db
        listed(vh, b, v_rows)
        vals = v_rows[...]
        w = weights[b, :MAXB].reshape(MAXB * BLK, BLK)
        dprobs = lax.dot_general(vals, db, LAST, preferred_element_type=F32)
        delta = jnp.sum(w.astype(F32) * dprobs, axis=0, keepdims=True)
        s = (probs[b] * (dprobs - delta)).astype(BF16)
        dscores[b, :MAXB] = s.reshape(MAXB, BLK, BLK)
        own_out[0, b] = lax.dot_general(w, vals, FIRST, preferred_element_type=F32).astype(BF16)
        own_out[1, b] = (
            lax.dot_general(s, k_rows[b], FIRST, preferred_element_type=F32) * SCALE
        ).astype(BF16)
        return 0

    lax.fori_loop(0, NZ, backward, 0)
    keeps = [spread(0, own_out.at[0], attn), spread(1, own_out.at[1], grad_q)]

    def group_grad(i, core, chip):
        tiles, rows = ((dscores, qh), (weights, d_cat))[i]
        base = core * (NX * NZ) + chip * NZ
        for s in range(NZ):
            for b in range(NZ):
                lhs[i, pl.ds(s * BLK, BLK), pl.ds(b * BLK, BLK)] = tiles[b, where[b, base + s]]
        total = jnp.dot(
            lhs[i], rows[...].reshape(NZ * BLK, DH), preferred_element_type=F32
        )
        if i == 0:
            total = total * SCALE
        return total.reshape(NZ, BLK, DH)

    order = ((far, left, right, x), (far, right, left, x))
    ahead, back = (to_right, to_left), (to_left, to_right)
    sent = [[None] * NX, [None] * NX]
    moves = [[], []]

    def ship(i, n, device):
        moves[i].append(go(
            sums.at[i, n], x_in.at[i, n], ox_send.at[i, n], ox_recv.at[i, n], device
        ))

    for n in range(NX):
        for i in range(2):
            give[i, n] = group_grad(i, 1 - c, order[i][n]).astype(BF16)
            sent[i][n] = go(
                give.at[i, n], sib_in.at[i, n], oc_send.at[i, n], oc_recv.at[i, n], sibling
            )
        for i in range(2):
            total = group_grad(i, c, order[i][n])
            sent[i][n].wait_recv()
            total = total + sib_in[i, n].astype(F32)
            if n == 2:
                moves[i][0].wait_recv()
                total = total + x_in[i, 0].astype(F32)
            if n == 3:
                moves[i][1].wait_recv()
                total = total + x_in[i, 1].astype(F32)
                moves[i][2].wait_recv()
                total = total + x_in[i, 2].astype(F32)
                final[i] = total.astype(BF16)
                keeps.append(spread(2 + i, final.at[i], (grad_k, grad_v)[i]))
            else:
                sums[i, n] = total.astype(BF16)
                ship(i, n, back[i] if n == 1 else ahead[i])
    for copy in parts:
        copy.wait_recv()
    for copy in keeps:
        copy.wait()
    for copy in copies:
        copy.wait_send()


def shards(queries, keys, values, d_out, block_lists, list_counts):
    hbm = pl.BlockSpec(memory_space=pl.ANY)
    smem = pl.BlockSpec(memory_space=pltpu.SMEM)
    dma = pltpu.SemaphoreType.DMA
    rows = BLK // (2 * NY)

    def vm(*shape, dtype=BF16):
        return pltpu.VMEM(shape, dtype)

    return pl.pallas_call(
        kernel,
        out_shape=(jax.ShapeDtypeStruct((BLK, GROUP * DH), BF16),) * 4,
        in_specs=[smem] * 2 + [hbm] * 4,
        out_specs=[hbm] * 4,
        scratch_shapes=[
            vm(NPOS, BLK, DH), vm(NPOS, BLK, DH), vm(NZ, BLK, DH), vm(NZ, NY, 2, rows, DH),
            vm(NY, rows, 2 * GROUP * DH), pltpu.SMEM((NZ, NPOS), jnp.int32),
            vm(NZ, MAXB * BLK, DH), vm(MAXB * BLK, DH), vm(NZ, MAXB * BLK, BLK, dtype=F32),
            vm(NZ, MAXB + 1, BLK, BLK), vm(NZ, MAXB + 1, BLK, BLK), vm(NZ, BLK, DH),
            vm(2, NZ, BLK, DH), vm(2, NZ * BLK, NZ * BLK), vm(2, NX, NZ, BLK, DH),
            vm(2, NX, NZ, BLK, DH), vm(2, 3, NZ, BLK, DH), vm(2, 3, NZ, BLK, DH),
            vm(2, NZ, BLK, DH),
            dma((3, NZ)), dma((3, NZ)), dma((2, 3, NZ)), dma((2, 3, NZ)), dma((2, NX)),
            dma((2, NX)), dma((NY,)), dma((NY,)), dma((2 * NZ,)), dma((2 * NZ,)),
            dma((4, NZ)), dma((4, NZ)), dma((2, 3)), dma((2, 3)), dma((2, NX)), dma((2, NX)),
            dma((9,)),
        ],
        compiler_params=pltpu.CompilerParams(
            collective_id=0, has_side_effects=True, vmem_limit_bytes=60 << 20
        ),
        name="attend",
    )(block_lists.T, list_counts, queries, keys, values, d_out)


def solution(mesh):
    spec = P("ctx", "head")
    return jax.shard_map(
        shards,
        mesh=mesh,
        in_specs=(spec, spec, spec, P(("ctx", "head"), None), P(), P()),
        out_specs=(spec,) * 4,
        check_vma=False,
    )
```

time: 359 us -> 62.6 us (0.17)
  blocking collectives: 155 us -> 0 us
  waiting for transfers between devices: 105 us -> 0 us
  Pallas kernels: 0 us -> 56.7 us
  matrix products: 37.4 us -> 0 us
  local copies, waits for them, and re-layouts: 31.3 us -> 4.16 us
  between operations: 13.9 us -> 0.65 us
  loops' own time: 13 us -> 0 us
    all_gather x2 -> x0, blocking collectives: 126 us -> none  [the longest x1 84.9 us: shards(): lax.all_gather(delta_rows, 'ctx', axis=1, tiled=True)]
    all_gather x4 -> x0, waiting for transfers between devices: 105 us -> none  [the longest x1 60.3 us: shards(): lax.all_gather(values, 'ctx', axis=0, tiled=True)]
    pallas_call x0 -> x1, Pallas kernels: none -> 56.7 us  [shards(): pl.pallas_call(kernel, out_shape=(jax.ShapeDtypeStruct((BLK, GROUP * DH),...]
    dot_general x16 -> x0, matrix products: 37.4 us -> none  [the longest x7 14.6 us: tile_scores(): jnp.einsum('qhd,khd->hqk', query_rows, key_rows, preferred_element_type=j...]
    all_to_all x1 -> x0, blocking collectives: 28.8 us -> none  [shards(): lax.all_to_all(d_out, 'head', split_axis=1, concat_axis=0, tiled=True)]
    another operation x3 -> x0, loops' own time: 13 us -> none  [the longest x1 4.35 us: listed_forward(): lax.fori_loop(0, list_count, first_pass, (start_max, start_total))]
    dynamic_slice x12 -> x0, local copies, waits for them, and re-layouts: 7.55 us -> none  [the longest x9 5.28 us: key_tile(): return lax.dynamic_slice_in_dim(heads_array, list_row[slot] * BLK, BLK, 0)]
    while x7 -> x0, local copies, waits for them, and re-layouts: 7.46 us -> none  [the longest x2 7.37 us: listed_forward(): lax.fori_loop(0, list_count, second_pass, jnp.zeros(q_block.shape, jnp.fl...]
  transfers between devices with their start and end apart: 4 -> 0, of which waited for: 2 -> 0; matrix products, arithmetic and copies ran while one was open for 13% -> 0% of each run, Pallas kernels for 0% -> 0%
where the time goes in v2:
time: 62.6 us; the launch traced here: 61.5 us
  Pallas kernels  56.7 us (91%)
  local copies, waits for them, and re-layouts  4.16 us (7%)
  between operations  0.65 us (1%)
    pallas_call x1, Pallas kernels, shards(): pl.pallas_call(kernel, out_shape=(jax.ShapeDtypeStruct((BLK, GROUP * DH),...  56.7 us
    unnamed x10, local copies, waits for them, and re-layouts  4.16 us

profile of v2, /device:TPU:1, one launch (start us, length us, event | category | flops | bytes accessed | tf_op | source)
XLA Modules:
  0.0 61.5 jit_solution(13036960126454578877)
XLA Ops:
  0.6 56.7 %attend.1 = (bf16[128,512]{1,0:T(8,128)(2,1)}, bf16[128,512]{1,0:T(8,128)(2,1)}, bf16[128,512]{1,0:T(8,128)(2,1)}, bf16[128,512]{1,0:T(8,128)(2,1)}) custom-call(s32[8,32]{1,0:T(8,128)} %bitcast.1, s32[32]{0:T(128)} %counts.1, bf16[128,512]{1,0:T(8,128)(2,1)} %q.1, bf16[128,512]{1,0:T(8,128)(2,1)} %k.1, bf16[128,512]{1,0:T(8,128)(2,1)} %v.1, bf16[8,8192]{1,0:T(8,128)(2,1)} %d.1), custom_call_target="tpu_custom_call" | custom-call | tf_op jit(solution)/shard_map/attend/pallas_call | solution.py:338
  57.4 0.0 copy-start.2
  57.4 1.6 %copy.14 = bf16[128,512]{1,0:T(8,128)(2,1)} copy(bf16[128,512]{1,0:T(8,128)(2,1)} %get-tuple-element.8) | data formatting | bytes 262144
  59.0 0.0 copy-done.2
  59.0 0.0 copy-start.1
  59.0 0.7 %copy.15 = bf16[128,512]{1,0:T(8,128)(2,1)} copy(bf16[128,512]{1,0:T(8,128)(2,1)S(1)} %copy-done.2) | data formatting | bytes 262144
  59.6 0.3 copy-done.1
  59.9 0.0 copy-start
  59.9 0.7 %copy.16 = bf16[128,512]{1,0:T(8,128)(2,1)} copy(bf16[128,512]{1,0:T(8,128)(2,1)S(1)} %copy-done.1) | data formatting | bytes 262144
  60.6 0.3 copy-done
  60.9 0.7 %copy.17 = bf16[128,512]{1,0:T(8,128)(2,1)} copy(bf16[128,512]{1,0:T(8,128)(2,1)S(1)} %copy-done) | data formatting | bytes 262144
Async XLA Ops:
  57.4 1.6 %copy-start.2 = (bf16[128,512]{1,0:T(8,128)(2,1)S(1)}, bf16[128,512]{1,0:T(8,128)(2,1)}, u32[]{:S(2)}) copy-start(bf16[128,512]{1,0:T(8,128)(2,1)} %get-tuple-element.9) | copy-start | bytes 393220
  59.0 1.0 %copy-start.1 = (bf16[128,512]{1,0:T(8,128)(2,1)S(1)}, bf16[128,512]{1,0:T(8,128)(2,1)}, u32[]{:S(2)}) copy-start(bf16[128,512]{1,0:T(8,128)(2,1)} %get-tuple-element.10) | copy-start | bytes 393220
  59.9 1.0 %copy-start = (bf16[128,512]{1,0:T(8,128)(2,1)S(1)}, bf16[128,512]{1,0:T(8,128)(2,1)}, u32[]{:S(2)}) copy-start(bf16[128,512]{1,0:T(8,128)(2,1)} %get-tuple-element.11) | copy-start | bytes 393220

commit v3 on v2

--- a/solution.py
+++ b/solution.py
@@ -59,9 +59,9 @@
 def kernel(
     lists, counts, q, k, v, d, attn, grad_q, grad_k, grad_v,
     kh, vh, qh, dh, d_rows, where, k_rows, v_rows, probs, weights, dscores, d_cat, own_out,
-    lhs, give, sib_in, sums, x_in, final,
+    lhs, give, sib_in, sums, x_in, final, stage, d_stage,
     z_send, z_recv, x_send, x_recv, c_send, c_recv, y_send, y_recv, d_send, d_recv,
-    oz_send, oz_recv, ox_send, ox_recv, oc_send, oc_recv, local,
+    oz_send, oz_recv, ox_send, ox_recv, oc_send, oc_recv, local, stage_sem, d_sem,
 ):
     x, z, c = coords()
     y, h = head_coords()
@@ -84,7 +84,6 @@
     barrier = pltpu.get_barrier_semaphore()
     for partner in partners:
         pl.semaphore_signal(barrier, inc=1, device_id=partner, device_id_type=MESH)
-    pl.semaphore_wait(barrier, len(partners))
     copies = []
 
     def go(*args):
@@ -97,11 +96,51 @@
         return copy
 
     ins, outs = (k, v, q), (kh, vh, qh)
+    places = (slot_of(x, z, c), slot_of(x, z, c), z)
+    own = [
+        keep(columns(ins[i], z * DH, DH), outs[i].at[places[i]], local.at[i]) for i in range(3)
+    ]
+    staging = [
+        [
+            keep(columns(ins[i], z_of[n] * DH, DH), stage.at[i, n - 1], stage_sem.at[i, n - 1])
+            for n in range(1, NZ)
+        ]
+        for i in range(3)
+    ]
+    d_stages = [
+        keep(
+            columns(d, ((y + r) % NY) * (2 * GROUP * DH), 2 * GROUP * DH),
+            d_rows.at[y] if r == 0 else d_stage.at[r - 1], d_sem.at[r],
+        )
+        for r in range(NY)
+    ]
+
+    def text_of(b):
+        return x * (NZ * NC) + b * NC + c
+
+    for b in range(NZ):
+        t = text_of(b)
+        count = counts[t]
+        live = [jnp.where(j < count, lists[j, t], -1) for j in range(MAXB)]
+
+        def find(pos, _):
+            p = ((pos // NZ) % NX) * (NZ * NC) + (pos % NZ) * NC + pos // (NX * NZ)
+            at = jnp.int32(MAXB)
+            for j in range(MAXB):
+                at = jnp.where(live[j] == p, j, at)
+            where[b, pos] = at
+            return 0
+
+        lax.fori_loop(0, NPOS, find, 0)
+        weights[b, MAXB] = jnp.zeros((BLK, BLK), BF16)
+        dscores[b, MAXB] = jnp.zeros((BLK, BLK), BF16)
+
+    pl.semaphore_wait(barrier, len(partners))
 
     def across(i, n):
-        place = slot_of(x, z, c) if i < 2 else z
+        staging[i][n - 1].wait()
         return go(
-            columns(ins[i], z_of[n] * DH, DH), outs[i].at[place],
+            stage.at[i, n - 1], outs[i].at[places[i]],
             z_send.at[i, n], z_recv.at[i, n], ctx_id(x, z_of[n], c),
         )
 
@@ -109,8 +148,7 @@
         to = (to_right, to_left, (to_right, to_left)[i])[role]
         chip = (x, x, (left, right)[i])[role]
         dst = outs[i].at[slot_of(chip, z_of[n], c)]
-        src = columns(ins[i], z * DH, DH) if role < 2 and n == 0 else dst
-        return go(src, dst, x_send.at[i, role, n], x_recv.at[i, role, n], to)
+        return go(dst, dst, x_send.at[i, role, n], x_recv.at[i, role, n], to)
 
     def over(i, m, chip):
         part = outs[i].at[pl.ds(c * (NX * NZ) + chip * NZ, NZ)]
@@ -139,59 +177,32 @@
             xs[i][2][n].wait_recv()
         sib[i].append(over(i, 3, far))
 
+    for n in range(1, NZ):
+        for i in range(2):
+            zs[i][n] = across(i, n)
     for i in range(2):
-        for n in range(1, NZ):
-            zs[i][n] = across(i, n)
+        own[i].wait()
         own_block(i, 0)
-    own = [
-        keep(columns(ins[i], z * DH, DH), outs[i].at[slot_of(x, z, c) if i < 2 else z], local.at[i])
-        for i in range(3)
-    ]
+    for r in range(1, NY):
+        d_stages[r].wait()
     ys = [
         go(
-            columns(d, ((y + r) % NY) * (2 * GROUP * DH), 2 * GROUP * DH), d_rows.at[y],
+            d_stage.at[r - 1], d_rows.at[y],
             y_send.at[r], y_recv.at[r], y_id(r),
         )
         for r in range(1, NY)
     ]
-    d_own = keep(columns(d, y * (2 * GROUP * DH), 2 * GROUP * DH), d_rows.at[y], local.at[3])
+
+    for n in range(1, NZ):
+        for i in range(2):
+            own_block(i, n)
+        for i in range(2):
+            pass_on(i, n - 1)
     for n in range(1, NZ):
         zs[2][n] = across(2, n)
-
-    def text_of(b):
-        return x * (NZ * NC) + b * NC + c
-
-    for b in range(NZ):
-        t = text_of(b)
-        count = counts[t]
-        live = [jnp.where(j < count, lists[j, t], -1) for j in range(MAXB)]
-
-        def find(pos, _):
-            p = ((pos // NZ) % NX) * (NZ * NC) + (pos % NZ) * NC + pos // (NX * NZ)
-            at = jnp.int32(MAXB)
-            for j in range(MAXB):
-                at = jnp.where(live[j] == p, j, at)
-            where[b, pos] = at
-            return 0
-
-        lax.fori_loop(0, NPOS, find, 0)
-        weights[b, MAXB] = jnp.zeros((BLK, BLK), BF16)
-        dscores[b, MAXB] = jnp.zeros((BLK, BLK), BF16)
-
-    own_block(0, 1)
-    pass_on(0, 0)
-    own_block(0, 2)
-    pass_on(0, 1)
-    own_block(0, 3)
-    own[0].wait()
-    sib[0].append(over(0, 0, x))
-    pass_on(0, 2)
-    own_block(1, 1)
-    pass_on(0, 3)
-    sib[0].append(over(0, 1, left))
-    pass_on(1, 0)
-    own_block(1, 2)
-    d_own.wait()
+    for i in range(2):
+        sib[i].append(over(i, 0, x))
+    d_stages[0].wait()
     for copy in ys:
         copy.wait_recv()
     ds = []
@@ -205,11 +216,11 @@
             else:
                 m = flip * NZ + n
                 ds.append(go(part, dst, d_send.at[m], d_recv.at[m], z_id(n, flip)))
-    own_block(1, 3)
-    own[1].wait()
-    sib[1].append(over(1, 0, x))
-    pass_on(1, 1)
+    for i in range(2):
+        pass_on(i, NZ - 1)
+        sib[i].append(over(i, 1, (left, right)[i]))
     rest(0)
+    rest(1)
     own[2].wait()
     for copy in zs[2][1:] + sib[0]:
         copy.wait_recv()
@@ -231,14 +242,8 @@
         probs[b] = p
         weights[b, :MAXB] = p.astype(BF16).reshape(MAXB, BLK, BLK)
 
-    softmax(0)
-    pass_on(1, 2)
-    softmax(1)
-    pass_on(1, 3)
-    sib[1].append(over(1, 1, right))
-    softmax(2)
-    rest(1)
-    softmax(3)
+    for b in range(NZ):
+        softmax(b)
     d_keep.wait()
     for copy in sib[1] + ds:
         copy.wait_recv()
@@ -326,6 +331,15 @@
         copy.wait_send()
 
 
+def hand_out(*refs):
+    ins, outs, sems = refs[:4], refs[4:8], refs[8]
+    copies = [pltpu.make_async_copy(ins[i], outs[i], sems.at[i]) for i in range(4)]
+    for copy in copies:
+        copy.start()
+    for copy in copies:
+        copy.wait()
+
+
 def shards(queries, keys, values, d_out, block_lists, list_counts):
     hbm = pl.BlockSpec(memory_space=pl.ANY)
     smem = pl.BlockSpec(memory_space=pltpu.SMEM)
@@ -335,7 +349,7 @@
     def vm(*shape, dtype=BF16):
         return pltpu.VMEM(shape, dtype)
 
-    return pl.pallas_call(
+    in_place = pl.pallas_call(
         kernel,
         out_shape=(jax.ShapeDtypeStruct((BLK, GROUP * DH), BF16),) * 4,
         in_specs=[smem] * 2 + [hbm] * 4,
@@ -347,17 +361,28 @@
             vm(NZ, MAXB + 1, BLK, BLK), vm(NZ, MAXB + 1, BLK, BLK), vm(NZ, BLK, DH),
             vm(2, NZ, BLK, DH), vm(2, NZ * BLK, NZ * BLK), vm(2, NX, NZ, BLK, DH),
             vm(2, NX, NZ, BLK, DH), vm(2, 3, NZ, BLK, DH), vm(2, 3, NZ, BLK, DH),
-            vm(2, NZ, BLK, DH),
+            vm(2, NZ, BLK, DH), vm(3, NZ - 1, BLK, DH), vm(NY - 1, rows, 2 * GROUP * DH),
             dma((3, NZ)), dma((3, NZ)), dma((2, 3, NZ)), dma((2, 3, NZ)), dma((2, NX)),
             dma((2, NX)), dma((NY,)), dma((NY,)), dma((2 * NZ,)), dma((2 * NZ,)),
             dma((4, NZ)), dma((4, NZ)), dma((2, 3)), dma((2, 3)), dma((2, NX)), dma((2, NX)),
-            dma((9,)),
+            dma((9,)), dma((3, NZ - 1)), dma((NY,)),
         ],
         compiler_params=pltpu.CompilerParams(
-            collective_id=0, has_side_effects=True, vmem_limit_bytes=60 << 20
+            collective_id=0, has_side_effects=True, vmem_limit_bytes=40 << 20
         ),
         name="attend",
-    )(block_lists.T, list_counts, queries, keys, values, d_out)
+    )(*(
+        pltpu.with_memory_space_constraint(a, pltpu.HBM)
+        for a in (block_lists.T, list_counts, queries, keys, values, d_out)
+    ))
+    return pl.pallas_call(
+        hand_out,
+        out_shape=(jax.ShapeDtypeStruct((BLK, GROUP * DH), BF16),) * 4,
+        in_specs=[pl.BlockSpec(memory_space=pltpu.VMEM)] * 4,
+        out_specs=[hbm] * 4,
+        scratch_shapes=[dma((4,))],
+        name="hand_out",
+    )(*(pltpu.with_memory_space_constraint(a, pltpu.VMEM) for a in in_place))
 
 
 def solution(mesh):

time: 62.6 us -> 57.1 us (0.912); the launches traced: 61.5 us -> 56.9 us
  local copies, waits for them, and re-layouts: 4.16 us -> 0 us
    unnamed x10 -> x0, local copies, waits for them, and re-layouts: 4.16 us -> none
    pallas_call x1, Pallas kernels: 56.7 us -> 55.5 us  [shards(): pl.pallas_call(kernel, out_shape=(jax.ShapeDtypeStruct((BLK, GROUP * DH),...]
    pallas_call x0 -> x1, Pallas kernels: none -> 0.82 us  [shards(): pl.pallas_call(hand_out, out_shape=(jax.ShapeDtypeStruct((BLK, GROUP * DH...]
where the time goes in v3:
time: 57.1 us; the launch traced here: 56.9 us
  Pallas kernels  56.3 us (99%)
  between operations  0.64 us (1%)
    pallas_call x1, Pallas kernels, shards(): pl.pallas_call(kernel, out_shape=(jax.ShapeDtypeStruct((BLK, GROUP * DH),...  55.5 us

profile of v3, /device:TPU:1, one launch (start us, length us, event | category | flops | bytes accessed | tf_op | source)
XLA Modules:
  0.0 56.9 jit_solution(10659312063243048916)
XLA Ops:
  0.6 55.5 %attend.1 = (bf16[128,512]{1,0:T(8,128)(2,1)S(1)}, bf16[128,512]{1,0:T(8,128)(2,1)S(1)}, bf16[128,512]{1,0:T(8,128)(2,1)S(1)}, bf16[128,512]{1,0:T(8,128)(2,1)S(1)}) custom-call(s32[8,32]{1,0:T(8,128)} %bitcast.1, s32[32]{0:T(128)} %counts.1, bf16[128,512]{1,0:T(8,128)(2,1)} %q.1, bf16[128,512]{1,0:T(8,128)(2,1)} %k.1, bf16[128,512]{1,0:T(8,128)(2,1)} %v.1, ...), custom_call_target="tpu_custom_call" | custom-call | tf_op jit(solution)/shard_map/attend/pallas_call | solution.py:352
  56.1 0.8 %hand_out.1 = (bf16[128,512]{1,0:T(8,128)(2,1)}, bf16[128,512]{1,0:T(8,128)(2,1)}, bf16[128,512]{1,0:T(8,128)(2,1)}, bf16[128,512]{1,0:T(8,128)(2,1)}) custom-call(bf16[128,512]{1,0:T(8,128)(2,1)S(1)} %get-tuple-element.8.refs_0_, bf16[128,512]{1,0:T(8,128)(2,1)S(1)} %get-tuple-element.9.refs_1_, bf16[128,512]{1,0:T(8,128)(2,1)S(1)} %get-tuple-element.10.refs_2_, ...), custom_call_target="tpu_custom_call" | custom-call | tf_op jit(solution)/shard_map/hand_out/pallas_call | solution.py:378

commit v4 on v3

--- a/solution.py
+++ b/solution.py
@@ -58,8 +58,8 @@
 
 def kernel(
     lists, counts, q, k, v, d, attn, grad_q, grad_k, grad_v,
-    kh, vh, qh, dh, d_rows, where, k_rows, v_rows, probs, weights, dscores, d_cat, own_out,
-    lhs, give, sib_in, sums, x_in, final, stage, d_stage,
+    kh, vh, qh, dh, d_rows, where, k_rows, v_rows, probs, weights, shares, d_cat, own_out,
+    give, sib_in, sums, x_in, final, stage, d_stage,
     z_send, z_recv, x_send, x_recv, c_send, c_recv, y_send, y_recv, d_send, d_recv,
     oz_send, oz_recv, ox_send, ox_recv, oc_send, oc_recv, local, stage_sem, d_sem,
 ):
@@ -67,6 +67,7 @@
     y, h = head_coords()
     right, left, far = (x + 1) % NX, (x + 3) % NX, (x + 2) % NX
     to_right, to_left, sibling = ctx_id(right, z, c), ctx_id(left, z, c), ctx_id(x, z, 1 - c)
+    to_far = ctx_id(far, z, c)
     z_of = z_order(z)
 
     def z_id(n, flip):
@@ -77,7 +78,7 @@
 
     partners = (
         [ctx_id(x, z_of[n], c) for n in range(1, NZ)]
-        + [to_right, to_left, sibling]
+        + [to_right, to_left, to_far, sibling]
         + [y_id(r) for r in range(1, NY)]
         + [z_id(n, 1) for n in range(NZ)]
     )
@@ -132,8 +133,8 @@
             return 0
 
         lax.fori_loop(0, NPOS, find, 0)
-        weights[b, MAXB] = jnp.zeros((BLK, BLK), BF16)
-        dscores[b, MAXB] = jnp.zeros((BLK, BLK), BF16)
+        for i in range(2):
+            shares[i, b, MAXB] = jnp.zeros((BLK, DH), F32)
 
     pl.semaphore_wait(barrier, len(partners))
 
@@ -145,10 +146,11 @@
         )
 
     def along(i, n, role):
-        to = (to_right, to_left, (to_right, to_left)[i])[role]
-        chip = (x, x, (left, right)[i])[role]
-        dst = outs[i].at[slot_of(chip, z_of[n], c)]
-        return go(dst, dst, x_send.at[i, role, n], x_recv.at[i, role, n], to)
+        passed = i == 1 and role == 2
+        chip = (left, right)[n // 2] if passed else x
+        to = (to_right, to_left)[n // 2] if passed else (to_right, to_left, to_far)[role]
+        part = outs[i].at[slot_of(chip, z_of[n], c)]
+        return go(part, part, x_send.at[i, role, n], x_recv.at[i, role, n], to)
 
     def over(i, m, chip):
         part = outs[i].at[pl.ds(c * (NX * NZ) + chip * NZ, NZ)]
@@ -161,47 +163,37 @@
     def own_block(i, n):
         if n > 0:
             zs[i][n].wait_recv()
-        for role in range(2):
+        for role in (2, 0, 1) if i == 0 else (0, 1):
             xs[i][role][n] = along(i, n, role)
 
-    def pass_on(i, n):
-        xs[i][i][n].wait_recv()
-        xs[i][2][n] = along(i, n, 2)
-
-    def rest(i):
-        other = 1 - i
+    def pass_on(n):
+        xs[1][n // 2][n].wait_recv()
+        xs[1][2][n] = along(1, n, 2)
+
+    def share(i, m):
         for n in range(NZ):
-            xs[i][other][n].wait_recv()
-        sib[i].append(over(i, 2, (right, left)[i]))
-        for n in range(NZ):
-            xs[i][2][n].wait_recv()
-        sib[i].append(over(i, 3, far))
+            if m > 0 and not (i == 1 and m - 1 == n // 2):
+                xs[i][m - 1][n].wait_recv()
+        sib[i].append(over(i, m, (x, left, right, far)[m]))
 
     for n in range(1, NZ):
-        for i in range(2):
-            zs[i][n] = across(i, n)
-    for i in range(2):
-        own[i].wait()
-        own_block(i, 0)
+        zs[0][n] = across(0, n)
+    own[0].wait()
+    own_block(0, 0)
+    ys = []
     for r in range(1, NY):
         d_stages[r].wait()
-    ys = [
-        go(
-            d_stage.at[r - 1], d_rows.at[y],
-            y_send.at[r], y_recv.at[r], y_id(r),
-        )
-        for r in range(1, NY)
-    ]
-
-    for n in range(1, NZ):
-        for i in range(2):
-            own_block(i, n)
-        for i in range(2):
-            pass_on(i, n - 1)
+        ys.append(go(d_stage.at[r - 1], d_rows.at[y], y_send.at[r], y_recv.at[r], y_id(r)))
     for n in range(1, NZ):
         zs[2][n] = across(2, n)
-    for i in range(2):
-        sib[i].append(over(i, 0, x))
+    own_block(0, 1)
+    own[1].wait()
+    own_block(1, 0)
+    for n in range(1, NZ):
+        zs[1][n] = across(1, n)
+    own_block(0, 2)
+    own_block(0, 3)
+    share(0, 0)
     d_stages[0].wait()
     for copy in ys:
         copy.wait_recv()
@@ -216,11 +208,15 @@
             else:
                 m = flip * NZ + n
                 ds.append(go(part, dst, d_send.at[m], d_recv.at[m], z_id(n, flip)))
-    for i in range(2):
-        pass_on(i, NZ - 1)
-        sib[i].append(over(i, 1, (left, right)[i]))
-    rest(0)
-    rest(1)
+    pass_on(0)
+    own_block(1, 1)
+    share(0, 1)
+    share(0, 2)
+    own_block(1, 2)
+    own_block(1, 3)
+    share(1, 0)
+    share(0, 3)
+    pass_on(1)
     own[2].wait()
     for copy in zs[2][1:] + sib[0]:
         copy.wait_recv()
@@ -240,13 +236,21 @@
         e = jnp.exp2((scores - top) * (SCALE * LOG2E))
         p = e * (1.0 / jnp.sum(e, axis=0, keepdims=True))
         probs[b] = p
-        weights[b, :MAXB] = p.astype(BF16).reshape(MAXB, BLK, BLK)
-
+        weights[b] = p.astype(BF16).reshape(MAXB, BLK, BLK)
+
+    softmax(0)
+    pass_on(2)
+    pass_on(3)
+    softmax(1)
+    share(1, 1)
+    share(1, 2)
+    softmax(2)
+    softmax(3)
+    d_keep.wait()
+    for copy in ds:
+        copy.wait_recv()
     for b in range(NZ):
-        softmax(b)
-    d_keep.wait()
-    for copy in sib[1] + ds:
-        copy.wait_recv()
+        d_cat[b] = dh[b].astype(F32).reshape(BLK, DH).astype(BF16)
 
     parts = []
 
@@ -256,76 +260,119 @@
                 src.at[z_of[n]], columns(out, z * DH, DH), oz_send.at[m, n], oz_recv.at[m, n],
                 ctx_id(x, z_of[n], c),
             ))
-        return keep(src.at[z], columns(out, z * DH, DH), local.at[5 + m])
-
-    def backward(b, _):
-        db = dh[b].astype(F32).reshape(BLK, DH).astype(BF16)
-        d_cat[b] = db
+        parts_own.append(keep(src.at[z], columns(out, z * DH, DH), local.at[5 + m]))
+
+    parts_own = []
+
+    def backward(b):
+        db = d_cat[b]
         listed(vh, b, v_rows)
         vals = v_rows[...]
-        w = weights[b, :MAXB].reshape(MAXB * BLK, BLK)
+        w = weights[b].reshape(MAXB * BLK, BLK)
         dprobs = lax.dot_general(vals, db, LAST, preferred_element_type=F32)
         delta = jnp.sum(w.astype(F32) * dprobs, axis=0, keepdims=True)
         s = (probs[b] * (dprobs - delta)).astype(BF16)
-        dscores[b, :MAXB] = s.reshape(MAXB, BLK, BLK)
+        shares[0, b, :MAXB] = (
+            jnp.dot(s, qh[b], preferred_element_type=F32) * SCALE
+        ).reshape(MAXB, BLK, DH)
         own_out[0, b] = lax.dot_general(w, vals, FIRST, preferred_element_type=F32).astype(BF16)
         own_out[1, b] = (
             lax.dot_general(s, k_rows[b], FIRST, preferred_element_type=F32) * SCALE
         ).astype(BF16)
-        return 0
-
-    lax.fori_loop(0, NZ, backward, 0)
-    keeps = [spread(0, own_out.at[0], attn), spread(1, own_out.at[1], grad_q)]
-
-    def group_grad(i, core, chip):
-        tiles, rows = ((dscores, qh), (weights, d_cat))[i]
-        base = core * (NX * NZ) + chip * NZ
+
+    def block_grad(i, core, chip, s):
+        p = slot_of(chip, s, core)
+        total = shares[i, 0, where[0, p]]
+        for b in range(1, NZ):
+            total = total + shares[i, b, where[b, p]]
+        return total
+
+    chips = (far, left, right, x)
+    halves = (range(NZ // 2), range(NZ // 2, NZ))
+    given = [[None] * NX, [None] * NX]
+    moves = [{}, {}]
+
+    def give_sibling(i, n):
         for s in range(NZ):
-            for b in range(NZ):
-                lhs[i, pl.ds(s * BLK, BLK), pl.ds(b * BLK, BLK)] = tiles[b, where[b, base + s]]
-        total = jnp.dot(
-            lhs[i], rows[...].reshape(NZ * BLK, DH), preferred_element_type=F32
+            give[i, n, s] = block_grad(i, 1 - c, chips[n], s).astype(BF16)
+        given[i][n] = go(
+            give.at[i, n], sib_in.at[i, n], oc_send.at[i, n], oc_recv.at[i, n], sibling
         )
-        if i == 0:
-            total = total * SCALE
-        return total.reshape(NZ, BLK, DH)
-
-    order = ((far, left, right, x), (far, right, left, x))
-    ahead, back = (to_right, to_left), (to_left, to_right)
-    sent = [[None] * NX, [None] * NX]
-    moves = [[], []]
-
-    def ship(i, n, device):
-        moves[i].append(go(
-            sums.at[i, n], x_in.at[i, n], ox_send.at[i, n], ox_recv.at[i, n], device
-        ))
-
-    for n in range(NX):
-        for i in range(2):
-            give[i, n] = group_grad(i, 1 - c, order[i][n]).astype(BF16)
-            sent[i][n] = go(
-                give.at[i, n], sib_in.at[i, n], oc_send.at[i, n], oc_recv.at[i, n], sibling
+
+    def core_sum(i, n, s):
+        return block_grad(i, c, chips[n], s) + sib_in[i, n, s].astype(F32)
+
+    def ship(i, role, half, blocks, device):
+        for s in range(NZ // 2):
+            sums[i, role, half, s] = blocks(halves[half][s]).astype(BF16)
+        moves[i][role, half] = go(
+            sums.at[i, role, half], x_in.at[i, role, half],
+            ox_send.at[i, role, half], ox_recv.at[i, role, half], device,
+        )
+
+    def first_steps(i):
+        for n in range(NX):
+            give_sibling(i, n)
+        for n, role in ((0, 0), (2, 1), (1, 1)):
+            given[i][n].wait_recv()
+            for half, device in ((0, to_right), (1, to_left)):
+                if i == 0:
+                    ship(i, n, half, lambda s: core_sum(i, n, s), (to_far, to_left, to_right)[n])
+                elif role == 0:
+                    ship(i, 0, half, lambda s: core_sum(i, 0, s), device)
+                elif (n == 1) == (half == 0):
+                    ship(i, 1, half, lambda s: core_sum(i, n, s), to_left if n == 1 else to_right)
+
+    def middle_steps(i):
+        for half, n, device in ((0, 2, to_right), (1, 1, to_left)):
+            moves[i][0, half].wait_recv()
+            ship(
+                i, 2, half,
+                lambda s: core_sum(i, n, s) + x_in[i, 0, half, s % (NZ // 2)].astype(F32), device,
             )
-        for i in range(2):
-            total = group_grad(i, c, order[i][n])
-            sent[i][n].wait_recv()
-            total = total + sib_in[i, n].astype(F32)
-            if n == 2:
-                moves[i][0].wait_recv()
-                total = total + x_in[i, 0].astype(F32)
-            if n == 3:
-                moves[i][1].wait_recv()
-                total = total + x_in[i, 1].astype(F32)
-                moves[i][2].wait_recv()
-                total = total + x_in[i, 2].astype(F32)
-                final[i] = total.astype(BF16)
-                keeps.append(spread(2 + i, final.at[i], (grad_k, grad_v)[i]))
+
+    def last_steps(i):
+        given[i][3].wait_recv()
+        for role in range(3) if i == 0 else (1, 2):
+            for half in range(2):
+                moves[i][role, half].wait_recv()
+        out = (grad_k, grad_v)[i]
+        for n in range(NZ - 1, -1, -1):
+            s = z_of[n]
+            half, at = s // (NZ // 2), s % (NZ // 2)
+            total = core_sum(i, 3, s)
+            for role in range(3) if i == 0 else (1, 2):
+                total = total + x_in[i, role, half, at].astype(F32)
+            final[i, s] = total.astype(BF16)
+            if n == 0:
+                parts_own.append(keep(final.at[i, z], columns(out, z * DH, DH), local.at[7 + i]))
             else:
-                sums[i, n] = total.astype(BF16)
-                ship(i, n, back[i] if n == 1 else ahead[i])
+                parts.append(go(
+                    final.at[i, s], columns(out, z * DH, DH), oz_send.at[2 + i, n],
+                    oz_recv.at[2 + i, n], ctx_id(x, s, c),
+                ))
+
+    for b in range(NZ):
+        shares[1, b, :MAXB] = jnp.dot(
+            weights[b].reshape(MAXB * BLK, BLK), d_cat[b], preferred_element_type=F32
+        ).reshape(MAXB, BLK, DH)
+    first_steps(1)
+    share(1, 3)
+    for copy in sib[1]:
+        copy.wait_recv()
+    backward(0)
+    middle_steps(1)
+    backward(1)
+    backward(2)
+    backward(3)
+    spread(0, own_out.at[0], attn)
+    spread(1, own_out.at[1], grad_q)
+    first_steps(0)
+    last_steps(1)
+    last_steps(0)
     for copy in parts:
         copy.wait_recv()
-    for copy in keeps:
+    for copy in parts_own:
         copy.wait()
     for copy in copies:
         copy.wait_send()
@@ -358,13 +405,13 @@
             vm(NPOS, BLK, DH), vm(NPOS, BLK, DH), vm(NZ, BLK, DH), vm(NZ, NY, 2, rows, DH),
             vm(NY, rows, 2 * GROUP * DH), pltpu.SMEM((NZ, NPOS), jnp.int32),
             vm(NZ, MAXB * BLK, DH), vm(MAXB * BLK, DH), vm(NZ, MAXB * BLK, BLK, dtype=F32),
-            vm(NZ, MAXB + 1, BLK, BLK), vm(NZ, MAXB + 1, BLK, BLK), vm(NZ, BLK, DH),
-            vm(2, NZ, BLK, DH), vm(2, NZ * BLK, NZ * BLK), vm(2, NX, NZ, BLK, DH),
-            vm(2, NX, NZ, BLK, DH), vm(2, 3, NZ, BLK, DH), vm(2, 3, NZ, BLK, DH),
+            vm(NZ, MAXB, BLK, BLK), vm(2, NZ, MAXB + 1, BLK, DH, dtype=F32), vm(NZ, BLK, DH),
+            vm(2, NZ, BLK, DH), vm(2, NX, NZ, BLK, DH),
+            vm(2, NX, NZ, BLK, DH), vm(2, 3, 2, NZ // 2, BLK, DH), vm(2, 3, 2, NZ // 2, BLK, DH),
             vm(2, NZ, BLK, DH), vm(3, NZ - 1, BLK, DH), vm(NY - 1, rows, 2 * GROUP * DH),
             dma((3, NZ)), dma((3, NZ)), dma((2, 3, NZ)), dma((2, 3, NZ)), dma((2, NX)),
             dma((2, NX)), dma((NY,)), dma((NY,)), dma((2 * NZ,)), dma((2 * NZ,)),
-            dma((4, NZ)), dma((4, NZ)), dma((2, 3)), dma((2, 3)), dma((2, NX)), dma((2, NX)),
+            dma((4, NZ)), dma((4, NZ)), dma((2, 3, 2)), dma((2, 3, 2)), dma((2, NX)), dma((2, NX)),
             dma((9,)), dma((3, NZ - 1)), dma((NY,)),
         ],
         compiler_params=pltpu.CompilerParams(

time: 57.1 us -> 53.7 us (0.940); the launches traced: 56.9 us -> 52.7 us
  Pallas kernels: 56.3 us -> 52.1 us
    pallas_call x1, Pallas kernels: 55.5 us -> 51.3 us  [shards(): pl.pallas_call(kernel, out_shape=(jax.ShapeDtypeStruct((BLK, GROUP * DH),...]
where the time goes in v4:
time: 53.7 us; the launch traced here: 52.7 us
  Pallas kernels  52.1 us (97%)
  between operations  0.64 us (1%)
    pallas_call x1, Pallas kernels, shards(): pl.pallas_call(kernel, out_shape=(jax.ShapeDtypeStruct((BLK, GROUP * DH),...  51.3 us

profile of v4, /device:TPU:1, one launch (start us, length us, event | category | flops | bytes accessed | tf_op | source)
XLA Modules:
  0.0 52.7 jit_solution(618019457395530521)
XLA Ops:
  0.6 51.3 %attend.1 = (bf16[128,512]{1,0:T(8,128)(2,1)S(1)}, bf16[128,512]{1,0:T(8,128)(2,1)S(1)}, bf16[128,512]{1,0:T(8,128)(2,1)S(1)}, bf16[128,512]{1,0:T(8,128)(2,1)S(1)}) custom-call(s32[8,32]{1,0:T(8,128)} %bitcast.1, s32[32]{0:T(128)} %counts.1, bf16[128,512]{1,0:T(8,128)(2,1)} %q.1, bf16[128,512]{1,0:T(8,128)(2,1)} %k.1, bf16[128,512]{1,0:T(8,128)(2,1)} %v.1, ...), custom_call_target="tpu_custom_call" | custom-call | tf_op jit(solution)/shard_map/attend/pallas_call | solution.py:399
  51.9 0.8 %hand_out.1 = (bf16[128,512]{1,0:T(8,128)(2,1)}, bf16[128,512]{1,0:T(8,128)(2,1)}, bf16[128,512]{1,0:T(8,128)(2,1)}, bf16[128,512]{1,0:T(8,128)(2,1)}) custom-call(bf16[128,512]{1,0:T(8,128)(2,1)S(1)} %get-tuple-element.8.refs_0_, bf16[128,512]{1,0:T(8,128)(2,1)S(1)} %get-tuple-element.9.refs_1_, bf16[128,512]{1,0:T(8,128)(2,1)S(1)} %get-tuple-element.10.refs_2_, ...), custom_call_target="tpu_custom_call" | custom-call | tf_op jit(solution)/shard_map/hand_out/pallas_call | solution.py:425

commit v5 on v4

--- a/solution.py
+++ b/solution.py
@@ -310,9 +310,11 @@
             ox_send.at[i, role, half], ox_recv.at[i, role, half], device,
         )
 
-    def first_steps(i):
+    def give_steps(i):
         for n in range(NX):
             give_sibling(i, n)
+
+    def first_steps(i):
         for n, role in ((0, 0), (2, 1), (1, 1)):
             given[i][n].wait_recv()
             for half, device in ((0, to_right), (1, to_left)):
@@ -356,25 +358,30 @@
         shares[1, b, :MAXB] = jnp.dot(
             weights[b].reshape(MAXB * BLK, BLK), d_cat[b], preferred_element_type=F32
         ).reshape(MAXB, BLK, DH)
+    give_steps(1)
     first_steps(1)
     share(1, 3)
     for copy in sib[1]:
         copy.wait_recv()
     backward(0)
-    middle_steps(1)
     backward(1)
     backward(2)
+    middle_steps(1)
     backward(3)
+    early = len(copies)
+    give_steps(0)
     spread(0, own_out.at[0], attn)
     spread(1, own_out.at[1], grad_q)
     first_steps(0)
+    for copy in copies[:early]:
+        copy.wait_send()
     last_steps(1)
     last_steps(0)
     for copy in parts:
         copy.wait_recv()
     for copy in parts_own:
         copy.wait()
-    for copy in copies:
+    for copy in copies[early:]:
         copy.wait_send()
 
 

time: 53.7 us -> 52.9 us (0.985); the launches traced: 52.7 us -> 52.6 us
  no operation moved by 1% of the time
where the time goes in v5:
time: 52.9 us; the launch traced here: 52.6 us
  Pallas kernels  51.9 us (98%)
  between operations  0.64 us (1%)
    pallas_call x1, Pallas kernels, shards(): pl.pallas_call(kernel, out_shape=(jax.ShapeDtypeStruct((BLK, GROUP * DH),...  51.1 us

profile of v5, /device:TPU:1, one launch (start us, length us, event | category | flops | bytes accessed | tf_op | source)
XLA Modules:
  0.0 52.6 jit_solution(16055589109128098856)
XLA Ops:
  0.6 51.1 %attend.1 = (bf16[128,512]{1,0:T(8,128)(2,1)S(1)}, bf16[128,512]{1,0:T(8,128)(2,1)S(1)}, bf16[128,512]{1,0:T(8,128)(2,1)S(1)}, bf16[128,512]{1,0:T(8,128)(2,1)S(1)}) custom-call(s32[8,32]{1,0:T(8,128)} %bitcast.1, s32[32]{0:T(128)} %counts.1, bf16[128,512]{1,0:T(8,128)(2,1)} %q.1, bf16[128,512]{1,0:T(8,128)(2,1)} %k.1, bf16[128,512]{1,0:T(8,128)(2,1)} %v.1, ...), custom_call_target="tpu_custom_call" | custom-call | tf_op jit(solution)/shard_map/attend/pallas_call | solution.py:406
  51.7 0.8 %hand_out.1 = (bf16[128,512]{1,0:T(8,128)(2,1)}, bf16[128,512]{1,0:T(8,128)(2,1)}, bf16[128,512]{1,0:T(8,128)(2,1)}, bf16[128,512]{1,0:T(8,128)(2,1)}) custom-call(bf16[128,512]{1,0:T(8,128)(2,1)S(1)} %get-tuple-element.8.refs_0_, bf16[128,512]{1,0:T(8,128)(2,1)S(1)} %get-tuple-element.9.refs_1_, bf16[128,512]{1,0:T(8,128)(2,1)S(1)} %get-tuple-element.10.refs_2_, ...), custom_call_target="tpu_custom_call" | custom-call | tf_op jit(solution)/shard_map/hand_out/pallas_call | solution.py:432
